TPU v7x, 32 devices: a whole 2x2x4 slice. The times are simulated.
32 devices in a mesh: crop: 1, row: 32 (over z, y, x, core).
Axes of the slice: x: 2, y: 2, z: 4, core: 2. Of those that a mesh axis runs over, the one named last changes fastest.
Arguments:
- queries: bfloat16 [128, 128, 128], P(('crop', 'row')), may hold values from -4 to 4
- keys: bfloat16 [128, 128, 128], P(('crop', 'row')), may hold values from -4 to 4
- values: bfloat16 [128, 128, 128], P(('crop', 'row')), may hold values from -6 to 6
- grads_out: bfloat16 [128, 128, 128], P(('crop', 'row')), may hold values from -96 to 96
- log_norm: float32 [128, 4, 128], P(('crop', 'row')), may hold values from -90 to 102, as said below
- bias: bfloat16 [128, 4, 128], P(('crop', 'row')), may hold values from -4 to 4
Outputs:
- query_grad: bfloat16 [128, 128, 128], P(('crop', 'row'))
- key_grad: bfloat16 [128, 128, 128], P(('crop', 'row'))
- value_grad: bfloat16 [128, 128, 128], P(('crop', 'row'))
- bias_grad: float32 [128, 4, 128], P(('crop', 'row'))
Inputs may be any that keep to these rules, and one draw needn't show every extreme that they name: log_norm[i, h, j] is the logarithm of the sum over k of exp(scores[i, h, j, k]), scores computed from the given queries, keys and bias.
All inputs are finite; a program needn't handle non-finite values.
Results may differ from a plain program's by a relative error of at most 0.0051.
Values may be sent and summed in bfloat16 or wider, within the bound.
No kernel may reach another device: no remote copies, remote signals or barrier semaphores. Data moves between devices by JAX's collectives and lax.ppermute only.
A program may use at most 64 MiB of HBM per device.

v0:
```python
import math

import jax
import jax.numpy as jnp
from jax import lax
from jax.sharding import PartitionSpec as P


def block_terms(arrays, bias_rows, first_row):
    queries, keys, values, grads_out, log_norm, head_count = arrays
    local_rows, length, pair_width = queries.shape
    head_width = pair_width // head_count
    row_count = bias_rows.shape[0]
    score_scale = head_width ** (-0.5)
    query_block = lax.dynamic_slice_in_dim(queries, first_row, row_count, 1).reshape(
        local_rows, row_count, head_count, head_width
    )
    grad_block = lax.dynamic_slice_in_dim(grads_out, first_row, row_count, 1).reshape(
        local_rows, row_count, head_count, head_width
    )
    key_heads = keys.reshape(local_rows, length, head_count, head_width)
    value_heads = values.reshape(local_rows, length, head_count, head_width)
    norm_block = lax.dynamic_slice_in_dim(log_norm, first_row, row_count, 2)
    scores = (
        jnp.einsum("rjhd,rkhd->rhjk", query_block, key_heads, preferred_element_type=jnp.float32)
        * score_scale
    )
    scores = scores + jnp.transpose(bias_rows, (1, 0, 2))[None].astype(jnp.float32)
    weights = jnp.exp(scores - norm_block[..., None])
    weight_grads = jnp.einsum(
        "rjhd,rkhd->rhjk", grad_block, value_heads, preferred_element_type=jnp.float32
    )
    centre = jnp.sum(weights * weight_grads, axis=-1, keepdims=True)
    score_grads = weights * (weight_grads - centre)
    return (query_block, grad_block, key_heads, weights, score_grads, score_scale)


def block_grads(arrays, bias_rows, first_row):
    query_block, grad_block, key_heads, weights, score_grads, score_scale = block_terms(
        arrays, bias_rows, first_row
    )
    local_rows, row_count, head_count, head_width = query_block.shape
    length = key_heads.shape[1]
    weights_low = weights.astype(jnp.bfloat16)
    grads_low = score_grads.astype(jnp.bfloat16)
    query_part = (
        jnp.einsum("rhjk,rkhd->rjhd", grads_low, key_heads, preferred_element_type=jnp.float32)
        * score_scale
    )
    key_part = (
        jnp.einsum("rhjk,rjhd->rkhd", grads_low, query_block, preferred_element_type=jnp.float32)
        * score_scale
    )
    value_part = jnp.einsum(
        "rhjk,rjhd->rkhd", weights_low, grad_block, preferred_element_type=jnp.float32
    )
    bias_part = jnp.transpose(jnp.sum(score_grads, axis=0), (1, 0, 2))
    pair_width = head_count * head_width
    return (
        query_part.reshape(local_rows, row_count, pair_width),
        key_part.reshape(local_rows, length, pair_width),
        value_part.reshape(local_rows, length, pair_width),
        bias_part,
    )


def sweep(arrays, bias_rows, running):
    total_rows = bias_rows.shape[0]
    block_rows = math.gcd(total_rows, 64)

    def sweep_advance(block_index, state):
        offset = block_index * block_rows
        rows_now = lax.dynamic_slice_in_dim(bias_rows, offset, block_rows, 0)
        query_part, key_part, value_part, bias_part = block_grads(arrays, rows_now, offset)
        query_sum, key_sum, value_sum, bias_sum = state
        query_sum = lax.dynamic_update_slice_in_dim(query_sum, query_part, offset, 1)
        key_sum = key_sum + key_part
        value_sum = value_sum + value_part
        return (query_sum, key_sum, value_sum, bias_sum)

    return lax.fori_loop(0, total_rows // block_rows, sweep_advance, running)


def gather_bias(bias):
    return lax.all_gather(bias, "row", axis=0, tiled=True)


def local(queries, keys, values, grads_out, log_norm, bias):
    head_count = bias.shape[1]
    local_rows, length, pair_width = queries.shape
    arrays = (queries, keys, values, grads_out, log_norm, head_count)
    blank = jnp.zeros((local_rows, length, pair_width), jnp.float32)
    gathered = gather_bias(bias)
    query_sum, key_sum, value_sum, unused = sweep(arrays, gathered, (blank, blank, blank, None))
    row_count = local_rows * lax.axis_size("row")
    block_rows = math.gcd(row_count, 64)

    def bias_advance(block_index, total):
        offset = block_index * block_rows
        rows_now = lax.dynamic_slice_in_dim(gathered, offset, block_rows, 0)
        score_grads = block_terms(arrays, rows_now, offset)[4]
        bias_part = jnp.transpose(jnp.sum(score_grads, axis=0), (1, 0, 2))
        return lax.dynamic_update_slice_in_dim(total, bias_part, offset, 0)

    start_total = jnp.zeros((row_count, head_count, length), jnp.float32)
    bias_grad = lax.psum_scatter(
        lax.fori_loop(0, row_count // block_rows, bias_advance, start_total),
        "row",
        scatter_dimension=0,
        tiled=True,
    )
    return (
        query_sum.astype(jnp.bfloat16),
        key_sum.astype(jnp.bfloat16),
        value_sum.astype(jnp.bfloat16),
        bias_grad,
    )


def solution(mesh):
    placed = (
        P(("crop", "row"), None, None),
        P(("crop", "row"), None, None),
        P(("crop", "row"), None, None),
        P(("crop", "row"), None, None),
        P(("crop", "row"), None, None),
        P(("crop", "row"), None, None),
    )
    return jax.shard_map(
        local,
        mesh=mesh,
        in_specs=placed,
        out_specs=(
            P(("crop", "row"), None, None),
            P(("crop", "row"), None, None),
            P(("crop", "row"), None, None),
            P(("crop", "row"), None, None),
        ),
        check_vma=False,
    )
```

profile of v0, /device:TPU:0, one launch (start us, length us, event | category | flops | bytes accessed | tf_op | source)
XLA Modules:
  0.0 189.5 jit_solution(9445011809489944761)
XLA Ops:
  7.2 0.0 all-reduce.3.cloned.1.call-start
  7.2 43.9 %all_gather.3 = bf16[128,4,128]{2,1,0:T(4,128)(2,1)S(1)} all-gather(bf16[4,4,128]{2,1,0:T(4,128)(2,1)} %param.15), channel_id=1, replica_groups=mesh['crop'=1,'row'=32] {'row'}, dimensions={0}, use_global_device_ids=true | all-gather | bytes 135168 | tf_op jit(solution)/shard_map/all_gather | solution.py:85
  51.1 0.0 copy-start.2
  51.1 0.9 copy-done.2
  52.0 0.0 copy-start.3
  52.0 0.1 copy.22
  52.1 0.8 copy-done.3
  52.9 0.0 copy-start.4
  52.9 0.1 copy.23
  53.0 0.8 copy-done.4
  53.8 0.0 copy-start.5
  53.8 0.1 copy.25
  53.9 0.8 copy-done.5
  54.7 0.1 copy.26
  54.8 0.0 copy-start.1
  54.9 0.6 copy-done.1
  55.5 2.3 %while.31 = (s32[]{:T(128)}, f32[128,4,128]{2,1,0:T(4,128)S(1)}, bf16[4,128,128]{1,2,0:T(8,128)(2,1)S(1)}, bf16[4,128,128]{1,2,0:T(8,128)(2,1)S(1)}, bf16[128,4,...) while((s32[]{:T(128)}, f32[128,4,128]{2,1,0:T(4,128)S(1)}, ...), condition=%wide.region_6.0_spmd, body=%wide.region_3.0_spmd.sunk | while | flops 26084484 | bytes 2437299 | solution.py:107
  55.5 0.1 constant_dynamic-slice_fusion.12
  55.7 0.1 constant_dynamic-slice_fusion.13
  55.8 0.3 fusion.57
  56.1 0.4 fusion.58
  56.6 0.1 copy_dynamic-update-slice_fusion.2
  56.7 0.1 constant_dynamic-slice_fusion.12
  56.9 0.1 constant_dynamic-slice_fusion.13
  56.9 0.3 fusion.57
  57.3 0.4 fusion.58
  57.7 0.1 copy_dynamic-update-slice_fusion.2
  57.8 0.0 copy-start
  57.8 0.7 copy-done
  58.5 0.0 all-reduce.3.cloned.1.call-update
  58.6 4.6 %while.32 = (s32[]{:T(128)}, bf16[4,128,128]{2,1,0:T(8,128)(2,1)S(1)}, f32[4,128,128]{1,2,0:T(8,128)S(1)}, f32[4,128,128]{1,2,0:T(8,128)S(1)}, bf16[4,128,128]{1...) while((s32[]{:T(128)}, ...), condition=%wide.region_2.0_spmd.clone, body=%wide.region_0.0_spmd.clone.sunk | while | flops 43547652 | bytes 7622865 | solution.py:81
  58.6 0.1 constant_dynamic-slice_fusion.14
  58.7 0.3 fusion.69
  59.0 0.1 constant_dynamic-slice_fusion.16
  59.1 0.1 constant_dynamic-slice_fusion.15
  59.2 0.5 multiply_reduce_fusion.3
  59.7 0.2 multiply_convert_fusion.2
  59.9 0.2 convolution_multiply_fusion.7
  60.1 0.2 fusion.70
  60.3 0.1 bitcast_add_fusion.3
  60.5 0.2 convolution_multiply_fusion.6
  60.7 0.1 copy.44
  60.9 0.1 constant_dynamic-slice_fusion.14
  61.0 0.3 fusion.69
  61.3 0.1 constant_dynamic-slice_fusion.16
  61.4 0.1 constant_dynamic-slice_fusion.15
  61.5 0.5 multiply_reduce_fusion.3
  62.0 0.2 multiply_convert_fusion.2
  62.2 0.2 convolution_multiply_fusion.7
  62.4 0.2 fusion.70
  62.6 0.1 bitcast_add_fusion.3
  62.7 0.2 convolution_multiply_fusion.6
  63.0 0.1 copy.44
  63.1 0.0 copy-start.6
  63.2 0.8 copy.28
  63.9 0.0 copy-done.6
  63.9 0.8 copy.29
  64.7 116.7 %all-reduce.3.cloned.1.call-done = f32[128,4,128]{2,1,0:T(4,128)} async-done(((f32[128,4,128]{2,1,0:T(4,128)}), f32[128,4,128]{2,1,0:T(4,128)}) %all-reduce.3.cloned.1.call-update) | async-done | bytes 262160
  181.4 1.3 constant_dynamic-slice_fusion.6
  (11 shorter events, 0.2 us)
Async XLA Ops:
  7.2 174.2 %all-reduce.3.cloned.1.call-start = ((), (), s32[]{:S(2)}) async-start(), calls=%async_computation | async-start | bytes 524288
  51.1 0.9 copy-start.2
  52.0 0.9 copy-start.3
  52.9 0.9 copy-start.4
  53.8 0.9 copy-start.5
  54.8 0.7 copy-start.1
  57.8 0.7 copy-start
  63.1 0.8 copy-start.6
Sparse Core Ops, SparseCore 0:
  58.7 122.6 all-reduce.2
where the time goes:
time: 190 us
  waiting for transfers between devices  117 us (62%)
  blocking collectives  43.9 us (23%)
  between operations  14.1 us (7%)
  local copies, waits for them, and re-layouts  9.41 us (5%)
  matrix products  4.34 us (2%)
    unnamed x2, waiting for transfers between devices  117 us
    all_gather x1, blocking collectives, gather_bias(): return lax.all_gather(bias, 'row', axis=0, tiled=True)  43.9 us
    unnamed x20, local copies, waits for them, and re-layouts  6.37 us
  transfers between devices with their start and end apart: 1, of which 1 were waited for; matrix products, arithmetic and copies ran while one was open for 3% of the time, Pallas kernels for 0%

commit v1 on v0

v1 whole, which is shorter than its diff:
```python
import jax
import jax.numpy as jnp
from jax import lax
from jax.sharding import PartitionSpec as P


def gather_rows(block, devices):
    copies = jnp.broadcast_to(block[None], (devices,) + block.shape)
    return lax.all_to_all(copies, "row", 0, 0)


def scatter_sum(partial, devices):
    rows = partial.shape[0] // devices
    parts = partial.astype(jnp.bfloat16).reshape((devices, rows) + partial.shape[1:])
    received = lax.all_to_all(parts, "row", 0, 0)
    return jnp.sum(received.astype(jnp.float32), axis=0)


def local(queries, keys, values, grads_out, log_norm, bias):
    head_count = bias.shape[1]
    local_rows, length, pair_width = queries.shape
    head_width = pair_width // head_count
    devices = lax.axis_size("row")
    score_scale = head_width ** (-0.5)
    gathered = gather_rows(bias, devices).reshape(length, head_count, length)

    def heads(array):
        return array.reshape(local_rows, length, head_count, head_width)

    def product(form, left, right):
        return jnp.einsum(form, left, right, preferred_element_type=jnp.float32)

    scores = product("rjhd,rkhd->rhjk", heads(queries), heads(keys)) * score_scale
    scores = scores + jnp.transpose(gathered, (1, 0, 2))[None].astype(jnp.float32)
    weights = jnp.exp(scores - log_norm[..., None])
    weight_grads = product("rjhd,rkhd->rhjk", heads(grads_out), heads(values))
    centre = jnp.sum(weights * weight_grads, axis=-1, keepdims=True)
    score_grads = weights * (weight_grads - centre)
    bias_part = jnp.transpose(jnp.sum(score_grads, axis=0), (1, 0, 2))
    bias_grad = scatter_sum(bias_part, devices)
    weights_low = weights.astype(jnp.bfloat16)
    grads_low = score_grads.astype(jnp.bfloat16)
    query_grad = product("rhjk,rkhd->rjhd", grads_low, heads(keys)) * score_scale
    key_grad = product("rhjk,rjhd->rkhd", grads_low, heads(queries)) * score_scale
    value_grad = product("rhjk,rjhd->rkhd", weights_low, heads(grads_out))

    def joined(array):
        return array.reshape(local_rows, length, pair_width).astype(jnp.bfloat16)

    return joined(query_grad), joined(key_grad), joined(value_grad), bias_grad


def solution(mesh):
    placed = P(("crop", "row"), None, None)
    return jax.shard_map(
        local, mesh=mesh, in_specs=(placed,) * 6, out_specs=(placed,) * 4, check_vma=False
    )
```

time: 190 us -> 34 us (0.18)
  waiting for transfers between devices: 117 us -> 12 us
  blocking collectives: 43.9 us -> 0 us
  between operations: 14.1 us -> 0.74 us
  starting transfers between devices: 0.04 us -> 9.89 us
  matrix products: 4.34 us -> 1.86 us
    unnamed x2 -> x0, waiting for transfers between devices: 117 us -> none
    all_gather x1 -> x0, blocking collectives: 43.9 us -> none  [gather_bias(): return lax.all_gather(bias, 'row', axis=0, tiled=True)]
    all_to_all x0 -> x2, waiting for transfers between devices: none -> 12 us  [the longest x1 7.04 us: scatter_sum(): received = lax.all_to_all(parts, 'row', 0, 0)]
    all_to_all x0 -> x2, starting transfers between devices: none -> 9.89 us  [the longest x1 7.33 us: gather_rows(): return lax.all_to_all(copies, 'row', 0, 0)]
    unnamed x20 -> x19, local copies, waits for them, and re-layouts: 6.37 us -> 7.01 us
  transfers between devices with their start and end apart: 1 -> 2, of which waited for: 1 -> 2; matrix products, arithmetic and copies ran while one was open for 3% -> 6% of each run, Pallas kernels for 0% -> 0%
where the time goes in v1:
time: 34 us; the launch traced here: 33.7 us
  waiting for transfers between devices  12 us (35%)
  starting transfers between devices  9.89 us (29%)
  local copies, waits for them, and re-layouts  8.84 us (26%)
  matrix products  1.86 us (5%)
  between operations  0.74 us (2%)
    all_to_all x1, starting transfers between devices, gather_rows(): return lax.all_to_all(copies, 'row', 0, 0)  7.33 us
    all_to_all x1, waiting for transfers between devices, scatter_sum(): received = lax.all_to_all(parts, 'row', 0, 0)  7.04 us
    unnamed x19, local copies, waits for them, and re-layouts  7.01 us
    all_to_all x1, waiting for transfers between devices, gather_rows(): return lax.all_to_all(copies, 'row', 0, 0)  4.98 us
    all_to_all x1, starting transfers between devices, scatter_sum(): received = lax.all_to_all(parts, 'row', 0, 0)  2.57 us
    dot_general x5, matrix products, product(): return jnp.einsum(form, left, right, preferred_element_type=jnp.float32)  1.86 us
    reshape x1, local copies, waits for them, and re-layouts, scatter_sum(): partial.astype(jnp.bfloat16).reshape((devices, rows) + partial.shape[1:])  0.7 us
    broadcast_in_dim x1, local copies, waits for them, and re-layouts, gather_rows(): copies = jnp.broadcast_to(block[None], (devices,) + block.shape)  0.69 us
  transfers between devices with their start and end apart: 2, of which 2 were waited for; matrix products, arithmetic and copies ran while one was open for 6% of the time, Pallas kernels for 0%

profile of v1, /device:TPU:0, one launch (start us, length us, event | category | flops | bytes accessed | tf_op | source)
XLA Modules:
  0.0 33.7 jit_solution(1719025029906945391)
XLA Ops:
  0.6 0.7 %copy.83 = bf16[4,4,128]{2,0,1:T(4,128)(2,1)S(1)} copy(bf16[4,4,128]{2,1,0:T(4,128)(2,1)} %param.11) | data formatting | bytes 8192 | tf_op args[5]
  1.3 0.7 %broadcast_in_dim.2 = bf16[32,4,4,128]{3,1,2,0:T(4,128)(2,1)} broadcast(bf16[4,4,128]{2,0,1:T(4,128)(2,1)S(1)} %copy.83), dimensions={1,2,3} | broadcast | bytes 135168 | tf_op jit(solution)/shard_map/broadcast_in_dim | solution.py:8
  2.0 0.0 copy-start
  2.0 7.3 %all-to-all-start = ((bf16[32,4,4,128]{3,1,2,0:T(4,128)(2,1)}), bf16[32,4,4,128]{3,1,2,0:T(4,128)(2,1)S(1)}, u32[]{:S(2)}, u32[]{:S(2)}) async-start(bf16[32,4,4,128]{3,1,2,0:T(4,128)(2,1)} %broadcast_in_dim.2), calls=%async_computation | async-start | bytes 262144 | tf_op jit(solution)/shard_map/all_to_all | solution.py:9
  9.4 0.0 copy-done
  9.4 0.0 copy-start.1
  9.4 0.1 copy.81
  9.5 0.8 %copy-done.1 = bf16[4,128,128]{2,1,0:T(8,128)(2,1)S(1)} copy-done((bf16[4,128,128]{2,1,0:T(8,128)(2,1)S(1)}, bf16[4,128,128]{2,1,0:T(8,128)(2,1)}, u32[]{:S(2)}) %copy-start.1) | copy-done | bytes 131096
  10.3 0.0 copy-start.2
  10.3 0.1 copy.82
  10.4 0.8 %copy-done.2 = bf16[4,128,128]{2,1,0:T(8,128)(2,1)S(1)} copy-done((bf16[4,128,128]{2,1,0:T(8,128)(2,1)S(1)}, bf16[4,128,128]{2,1,0:T(8,128)(2,1)}, u32[]{:S(2)}) %copy-start.2) | copy-done | bytes 131096
  11.2 0.0 copy-start.3
  11.2 0.1 copy.88
  11.3 0.8 %copy-done.3 = bf16[4,128,128]{2,1,0:T(8,128)(2,1)S(1)} copy-done((bf16[4,128,128]{2,1,0:T(8,128)(2,1)S(1)}, bf16[4,128,128]{2,1,0:T(8,128)(2,1)}, u32[]{:S(2)}) %copy-start.3) | copy-done | bytes 131096
  12.1 0.1 copy.87
  12.2 0.4 %fusion.8 = f32[4,4,128,128]{2,3,1,0:T(8,128)S(1)} fusion(bf16[4,128,4,32]{1,3,2,0:T(8,128)(2,1)S(1)} %bitcast.29, bf16[4,128,4,32]{1,3,2,0:T(8,128)(2,1)S(1)} %bitcast.37), kind=kOutput, calls=%fused_computation.17 | convolution fusion | flops 16777216 | bytes 1310720 | tf_op jit(solution)/shard_map/rjhd,rkhd->rhjk/dot_general | solution.py:31
  12.6 5.0 %all-to-all-done = bf16[32,4,4,128]{3,1,2,0:T(4,128)(2,1)S(1)} async-done(((bf16[32,4,4,128]{3,1,2,0:T(4,128)(2,1)}), bf16[32,4,4,128]{3,1,2,0:T(4,128)(2,1)S(1)}, u32[]{:S(2)}, u32[]{:S(2)}) %all-to-all-start) | async-done | bytes 131104 | tf_op jit(solution)/shard_map/all_to_all | solution.py:9
  17.6 0.2 copy.85
  17.8 0.0 copy-start.4
  17.8 0.1 copy.86
  17.9 0.6 %copy-done.4 = f32[4,4,128]{2,1,0:T(4,128)S(1)} copy-done((f32[4,4,128]{2,1,0:T(4,128)S(1)}, f32[4,4,128]{2,1,0:T(4,128)}, u32[]{:S(2)}) %copy-start.4) | copy-done | bytes 8216
  18.5 0.5 %multiply_reduce_fusion = (f32[4,4,128]{2,1,0:T(4,128)S(1)}, f32[4,4,128,128]{2,3,1,0:T(8,128)S(1)}) fusion(f32[4,4,128,128]{2,3,1,0:T(8,128)S(1)} %fusion.8, f32[4,4,128]{2,1,0:T(4,128)S(1)} %copy-done.4, f32[4,128,128]{1,2,0:T(8,128)S(1)} %copy.86, bf16[4,128,4,32]{1,3,2,0:T(8,128)(2,1)S(1)} %bitcast.33, bf16[4,128,4,32]{1,3,2,0:T(8,128)(2,1)S(1)} %bitcast.31), kind=kOutput, calls=%fused_computation.10 | convolution fusion | flops 18085888 | bytes 2637824 | tf_op jit(solution)/shard_map/rjhd,rkhd->rhjk/dot_general | solution.py:31
  19.0 0.2 fusion.6
  19.2 0.4 %fusion.3 = bf16[4,4,128,32]{2,3,1,0:T(8,128)(2,1)S(1)} fusion(bf16[4,4,128,128]{2,3,1,0:T(8,128)(2,1)S(1)} %get-tuple-element.29, bf16[4,128,4,32]{1,3,2,0:T(8,128)(2,1)S(1)} %bitcast.34), kind=kOutput, calls=%fused_computation.6 | convolution fusion | flops 16908288 | bytes 786432 | tf_op jit(solution)/shard_map/rhjk,rjhd->rkhd/dot_general | solution.py:31
  19.6 0.3 fusion.4
  19.8 0.1 copy.92
  20.0 0.7 %copy.93 = bf16[32,4,4,128]{3,1,2,0:T(4,128)(2,1)} copy(bf16[32,4,4,128]{3,1,0,2:T(4,128)(2,1)S(1)} %bitcast.38) | data formatting | bytes 262144 | tf_op jit(solution)/shard_map/reshape | solution.py:14
  20.7 0.8 %copy.94 = bf16[4,128,128]{2,1,0:T(8,128)(2,1)} copy(bf16[4,128,128]{1,2,0:T(8,128)(2,1)S(1)} %bitcast.40) | data formatting | bytes 262144
  21.4 0.8 %copy.95 = bf16[4,128,128]{2,1,0:T(8,128)(2,1)} copy(bf16[4,128,128]{1,2,0:T(8,128)(2,1)S(1)} %bitcast.39) | data formatting | bytes 262144
  22.2 2.6 %all-to-all-start.1 = ((bf16[32,4,4,128]{3,1,2,0:T(4,128)(2,1)}), bf16[32,4,4,128]{3,1,2,0:T(4,128)(2,1)S(1)}, u32[]{:S(2)}, u32[]{:S(2)}) async-start(bf16[32,4,4,128]{3,1,2,0:T(4,128)(2,1)} %copy.93), calls=%async_computation.1 | async-start | bytes 262144 | tf_op jit(solution)/shard_map/all_to_all | solution.py:15
  24.8 0.4 %convolution_convert_fusion = bf16[4,4,128,32]{2,3,1,0:T(8,128)(2,1)S(1)} fusion(bf16[4,128,4,32]{1,3,2,0:T(8,128)(2,1)S(1)} %bitcast.30, f32[4,4,128,128]{2,3,1,0:T(8,128)S(1)} %get-tuple-element.31), kind=kOutput, calls=%fused_computation.8 | convolution fusion | flops 17104896 | bytes 1310720 | tf_op jit(solution)/shard_map/rhjk,rjhd->rkhd/dot_general | solution.py:31
  25.2 0.8 %copy.96 = bf16[4,128,128]{2,1,0:T(8,128)(2,1)} copy(bf16[4,128,128]{1,2,0:T(8,128)(2,1)S(1)} %bitcast.36) | data formatting | bytes 262144
  25.9 7.0 %all-to-all-done.1 = bf16[32,4,4,128]{3,1,2,0:T(4,128)(2,1)S(1)} async-done(((bf16[32,4,4,128]{3,1,2,0:T(4,128)(2,1)}), bf16[32,4,4,128]{3,1,2,0:T(4,128)(2,1)S(1)}, u32[]{:S(2)}, u32[]{:S(2)}) %all-to-all-start.1) | async-done | bytes 131104 | tf_op jit(solution)/shard_map/all_to_all | solution.py:15
  33.0 0.1 convert_reduce_fusion
  33.1 0.6 %copy.97 = f32[4,4,128]{2,1,0:T(4,128)} copy(f32[4,4,128]{2,0,1:T(4,128)S(1)} %convert_reduce_fusion) | data formatting | bytes 16384
  (1 shorter events, 0.0 us)
Async XLA Ops:
  2.0 7.3 %copy-start = (bf16[4,128,128]{2,1,0:T(8,128)(2,1)S(1)}, bf16[4,128,128]{2,1,0:T(8,128)(2,1)}, u32[]{:S(2)}) copy-start(bf16[4,128,128]{2,1,0:T(8,128)(2,1)} %param.6) | copy-start | bytes 393220
  2.0 15.5 %all-to-all-start = ((bf16[32,4,4,128]{3,1,2,0:T(4,128)(2,1)}), bf16[32,4,4,128]{3,1,2,0:T(4,128)(2,1)S(1)}, u32[]{:S(2)}, u32[]{:S(2)}) async-start(bf16[32,4,4,128]{3,1,2,0:T(4,128)(2,1)} %broadcast_in_dim.2), calls=%async_computation | async-start | bytes 262144 | tf_op jit(solution)/shard_map/all_to_all | solution.py:9
  9.4 0.9 %copy-start.1 = (bf16[4,128,128]{2,1,0:T(8,128)(2,1)S(1)}, bf16[4,128,128]{2,1,0:T(8,128)(2,1)}, u32[]{:S(2)}) copy-start(bf16[4,128,128]{2,1,0:T(8,128)(2,1)} %param.7) | copy-start | bytes 393220
  10.3 0.9 %copy-start.2 = (bf16[4,128,128]{2,1,0:T(8,128)(2,1)S(1)}, bf16[4,128,128]{2,1,0:T(8,128)(2,1)}, u32[]{:S(2)}) copy-start(bf16[4,128,128]{2,1,0:T(8,128)(2,1)} %param.8) | copy-start | bytes 393220
  11.2 0.9 %copy-start.3 = (bf16[4,128,128]{2,1,0:T(8,128)(2,1)S(1)}, bf16[4,128,128]{2,1,0:T(8,128)(2,1)}, u32[]{:S(2)}) copy-start(bf16[4,128,128]{2,1,0:T(8,128)(2,1)} %param.9) | copy-start | bytes 393220
  17.8 0.7 %copy-start.4 = (f32[4,4,128]{2,1,0:T(4,128)S(1)}, f32[4,4,128]{2,1,0:T(4,128)}, u32[]{:S(2)}) copy-start(f32[4,4,128]{2,1,0:T(4,128)} %param.10) | copy-start | bytes 24580
  22.2 10.8 %all-to-all-start.1 = ((bf16[32,4,4,128]{3,1,2,0:T(4,128)(2,1)}), bf16[32,4,4,128]{3,1,2,0:T(4,128)(2,1)S(1)}, u32[]{:S(2)}, u32[]{:S(2)}) async-start(bf16[32,4,4,128]{3,1,2,0:T(4,128)(2,1)} %copy.93), calls=%async_computation.1 | async-start | bytes 262144 | tf_op jit(solution)/shard_map/all_to_all | solution.py:15

commit v2 on v1

v2 whole, which is shorter than its diff:
```python
import functools

import jax
import jax.numpy as jnp
from jax import lax
from jax.experimental import pallas as pl
from jax.experimental.pallas import tpu as pltpu
from jax.sharding import PartitionSpec as P

NT = (((1,), (1,)), ((), ()))
TN = (((0,), (0,)), ((), ()))
LANES = 128


def product(left, right, form):
    return lax.dot_general(left, right, form, preferred_element_type=jnp.float32)


def head_lanes(shape, head, width):
    lane = lax.broadcasted_iota(jnp.int32, shape, len(shape) - 1)
    return (lane >= head * width) & (lane < (head + 1) * width)


def only_head(array, head, width):
    return jnp.where(head_lanes(array.shape, head, width), array, jnp.zeros_like(array))


def before_kernel(heads, q_ref, k_ref, v_ref, g_ref, norm_ref, e_ref, f_ref, a_ref):
    rows, _, channels = q_ref.shape
    width = channels // heads
    scale = width ** (-0.5)
    norms = jnp.transpose(norm_ref[...])
    for head in range(heads):
        total = None
        for row in range(rows):
            column = row * heads + head
            scores = product(only_head(q_ref[row], head, width), k_ref[row], NT) * scale
            e = jnp.exp(scores - norms[:, column : column + 1])
            f = e * product(only_head(g_ref[row], head, width), v_ref[row], NT)
            e_ref[row, head] = e
            f_ref[row, head] = f
            total = f if total is None else total + f
        a_ref[head] = total


def bias_factor(bias_ref, spread_ref):
    devices, block, length = bias_ref.shape
    factor = jnp.exp(bias_ref[...].reshape(devices * block, length).astype(jnp.float32))
    for piece in range(length // LANES):
        spread_ref[piece] = factor[:, piece * LANES : (piece + 1) * LANES]


def factor_of(spread_ref, head, heads, length):
    here = pl.ds(head, length, stride=heads)
    pieces = [spread_ref[piece, here, :] for piece in range(length // LANES)]
    return pieces[0] if len(pieces) == 1 else jnp.concatenate(pieces, axis=1)


def middle_kernel(bias_ref, e_ref, f_ref, a_ref, part_ref, spread_ref, sums_ref):
    rows, heads, length, _ = e_ref.shape
    bias_factor(bias_ref, spread_ref)
    for head in range(heads):
        factor = factor_of(spread_ref, head, heads, length)
        total = a_ref[head]
        for row in range(rows):
            centre = jnp.sum(factor * f_ref[row, head], axis=1, keepdims=True)
            total = total - centre * e_ref[row, head]
        total = factor * total
        for piece in range(length // LANES):
            lanes = total[:, piece * LANES : (piece + 1) * LANES]
            sums_ref[piece, pl.ds(head, length, stride=heads), :] = lanes
    for piece in range(length // LANES):
        lanes = sums_ref[piece].astype(jnp.bfloat16).reshape(part_ref.shape[:2] + (LANES,))
        part_ref[:, :, piece * LANES : (piece + 1) * LANES] = lanes


def after_kernel(
    bias_ref, e_ref, f_ref, q_ref, k_ref, g_ref, dq_ref, dk_ref, dv_ref, spread_ref, w_ref, s_ref
):
    rows, heads, length, _ = e_ref.shape
    width = q_ref.shape[2] // heads
    scale = width ** (-0.5)
    bias_factor(bias_ref, spread_ref)
    for row in range(rows):
        for head in range(heads):
            factor = factor_of(spread_ref, head, heads, length)
            e, f = e_ref[row, head], f_ref[row, head]
            centre = jnp.sum(factor * f, axis=1, keepdims=True)
            here = pl.ds(head * length, length)
            w_ref[here, :] = (factor * e).astype(jnp.bfloat16)
            s_ref[here, :] = (factor * (f - centre * e)).astype(jnp.bfloat16)
        grads = s_ref[...]
        total = None
        for head in range(heads):
            term = product(
                grads[head * length : (head + 1) * length],
                only_head(k_ref[row], head, width),
                (((1,), (0,)), ((), ())),
            )
            total = term if total is None else total + term
        dq_ref[row] = (total * scale).astype(jnp.bfloat16)
        stacked = jnp.concatenate([only_head(q_ref[row], h, width) for h in range(heads)], 0)
        dk_ref[row] = (product(grads, stacked, TN) * scale).astype(jnp.bfloat16)
        stacked = jnp.concatenate([only_head(g_ref[row], h, width) for h in range(heads)], 0)
        dv_ref[row] = product(w_ref[...], stacked, TN).astype(jnp.bfloat16)


def call(kernel, name, outputs, scratch=(), flops=0, limit=16 << 20):
    return pl.pallas_call(
        kernel,
        name=name,
        out_shape=outputs,
        scratch_shapes=scratch,
        compiler_params=pltpu.CompilerParams(vmem_limit_bytes=limit),
        cost_estimate=pl.CostEstimate(flops=flops, bytes_accessed=1 << 20, transcendentals=0),
    )


def local(queries, keys, values, grads_out, log_norm, bias):
    heads = bias.shape[1]
    rows, length, channels = queries.shape
    devices = lax.axis_size("row")
    shape, f32, bf16 = jax.ShapeDtypeStruct, jnp.float32, jnp.bfloat16
    block = (rows * heads, length)
    tiles = (rows, heads, length, length)
    copies = jnp.broadcast_to(bias.reshape(block)[None], (devices,) + block)
    gathered = lax.all_to_all(copies, "row", 0, 0)
    e, f, a = call(
        functools.partial(before_kernel, heads),
        "before",
        (shape(tiles, f32), shape(tiles, f32), shape(tiles[1:], f32)),
        flops=1 << 30,
    )(queries, keys, values, grads_out, log_norm.reshape(block))
    wide = pltpu.VMEM((length // LANES, length * heads, LANES), f32)
    part = call(
        middle_kernel, "middle", shape((devices,) + block, bf16), (wide, wide), flops=1 << 20
    )(gathered, e, f, a)
    received = lax.all_to_all(part, "row", 0, 0)
    narrow = pltpu.VMEM((length * heads, length), bf16)
    grads = call(
        after_kernel,
        "after",
        (shape(queries.shape, bf16),) * 3,
        (wide, narrow, narrow),
        flops=1 << 30,
    )(gathered, e, f, queries, keys, grads_out)
    bias_grad = jnp.sum(received.astype(f32), axis=0).reshape(bias.shape)
    return (*grads, bias_grad)


def solution(mesh):
    placed = P(("crop", "row"), None, None)
    return jax.shard_map(
        local, mesh=mesh, in_specs=(placed,) * 6, out_specs=(placed,) * 4, check_vma=False
    )
```

time: 34 us -> 30.5 us (0.90)
  local copies, waits for them, and re-layouts: 8.84 us -> 3.01 us
  Pallas kernels: 0 us -> 3.64 us
  matrix products: 1.86 us -> 0 us
    unnamed x19 -> x12, local copies, waits for them, and re-layouts: 7.01 us -> 1.61 us
    pallas_call x0 -> x3, Pallas kernels: none -> 3.64 us  [the longest x1 1.69 us: local(): call(after_kernel, 'after', (shape(queries.shape, bf16),) * 3, (wide, nar...]
    dot_general x5 -> x0, matrix products: 1.86 us -> none  [product(): return jnp.einsum(form, left, right, preferred_element_type=jnp.float32)]
    broadcast_in_dim x1, local copies, waits for them, and re-layouts: 0.69 us -> 1.39 us  [local(): copies = jnp.broadcast_to(bias.reshape(block)[None], (devices,) + block)]
    reshape x1 -> x0, local copies, waits for them, and re-layouts: 0.7 us -> none  [scatter_sum(): partial.astype(jnp.bfloat16).reshape((devices, rows) + partial.shape[1:])]
    convert_element_type x3 -> x0, local copies, waits for them, and re-layouts: 0.44 us -> none  [the longest x2 0.3 us: local(): jnp.transpose(gathered, (1, 0, 2))[None].astype(jnp.float32)]
    reduce_sum x2 -> x1, other arithmetic: 0.29 us -> 0.63 us  [local(): bias_grad = jnp.sum(received.astype(f32), axis=0).reshape(bias.shape)]
  transfers between devices with their start and end apart: 2 -> 2, of which waited for: 2 -> 2; matrix products, arithmetic and copies ran while one was open for 6% -> 0% of each run, Pallas kernels for 0% -> 9%
where the time goes in v2:
time: 30.5 us; the launch traced here: 30.2 us
  waiting for transfers between devices  12.2 us (40%)
  starting transfers between devices  10 us (33%)
  Pallas kernels  3.64 us (12%)
  local copies, waits for them, and re-layouts  3.01 us (10%)
  between operations  0.71 us (2%)
  other arithmetic  0.63 us (2%)
    all_to_all x1, starting transfers between devices, local(): gathered = lax.all_to_all(copies, 'row', 0, 0)  7.33 us
    all_to_all x1, waiting for transfers between devices, local(): received = lax.all_to_all(part, 'row', 0, 0)  6.5 us
    all_to_all x1, waiting for transfers between devices, local(): gathered = lax.all_to_all(copies, 'row', 0, 0)  5.68 us
    all_to_all x1, starting transfers between devices, local(): received = lax.all_to_all(part, 'row', 0, 0)  2.69 us
    pallas_call x1, Pallas kernels, local(): call(after_kernel, 'after', (shape(queries.shape, bf16),) * 3, (wide, nar...  1.69 us
    unnamed x12, local copies, waits for them, and re-layouts  1.61 us
    broadcast_in_dim x1, local copies, waits for them, and re-layouts, local(): copies = jnp.broadcast_to(bias.reshape(block)[None], (devices,) + block)  1.39 us
    pallas_call x1, Pallas kernels, local(): call(middle_kernel, 'middle', shape((devices,) + block, bf16), (wide, wid...  1.06 us
  transfers between devices with their start and end apart: 2, of which 2 were waited for; matrix products, arithmetic and copies ran while one was open for 0% of the time, Pallas kernels for 9%

profile of v2, /device:TPU:0, one launch (start us, length us, event | category | flops | bytes accessed | tf_op | source)
XLA Modules:
  0.0 30.2 jit_solution(16078570425022681575)
XLA Ops:
  0.6 0.0 copy-start.2
  0.6 1.4 %broadcast_in_dim.8 = bf16[32,16,128]{2,1,0:T(8,128)(2,1)} broadcast(bf16[16,128]{1,0:T(8,128)(2,1)} %bitcast.5), dimensions={1,2} | broadcast | bytes 135168 | tf_op jit(solution)/shard_map/broadcast_in_dim | solution.py:126
  2.0 0.0 copy-start
  2.0 0.0 copy-start.1
  2.0 7.3 %all-to-all-start = ((bf16[32,16,128]{2,1,0:T(8,128)(2,1)}), bf16[32,16,128]{2,1,0:T(8,128)(2,1)S(1)}, u32[]{:S(2)}, u32[]{:S(2)}) async-start(bf16[32,16,128]{2,1,0:T(8,128)(2,1)} %broadcast_in_dim.8), calls=%async_computation | async-start | bytes 262144 | tf_op jit(solution)/shard_map/all_to_all | solution.py:127
  9.4 0.0 copy-done.2
  9.4 0.0 copy-done
  9.4 0.0 copy-done.1
  9.4 0.0 copy-start.3
  9.4 0.9 %copy-done.3 = bf16[4,128,128]{2,1,0:T(8,128)(2,1)S(1)} copy-done((bf16[4,128,128]{2,1,0:T(8,128)(2,1)S(1)}, bf16[4,128,128]{2,1,0:T(8,128)(2,1)}, u32[]{:S(2)}) %copy-start.3) | copy-done | bytes 131096
  10.3 0.0 copy-start.5
  10.3 0.7 %copy-done.5 = f32[4,4,128]{2,1,0:T(4,128)S(1)} copy-done((f32[4,4,128]{2,1,0:T(4,128)S(1)}, f32[4,4,128]{2,1,0:T(4,128)}, u32[]{:S(2)}) %copy-start.5) | copy-done | bytes 8216
  11.0 0.9 %before.1 = (f32[4,4,128,128]{3,2,1,0:T(8,128)S(1)}, f32[4,4,128,128]{3,2,1,0:T(8,128)S(1)}, f32[4,128,128]{2,1,0:T(8,128)S(1)}) custom-call(bf16[4,128,128]{2,1,0:T(8,128)(2,1)S(1)} %copy-done.1, bf16[4,128,128]{2,1,0:T(8,128)(2,1)S(1)} %copy-done.2, bf16[4,128,128]{2,1,0:T(8,128)(2,1)S(1)} %copy-done, bf16[4,128,128]{2,1,0:T(8,128)(2,1)S(1)} %copy-done.3, ...), custom_call_target="tpu_custom_call" | custom-call | flops 1073741824 | bytes 1048576 | tf_op jit(solution)/shard_map/before/pallas_call | solution.py:128
  11.9 5.7 %all-to-all-done.bias_ref = bf16[32,16,128]{2,1,0:T(8,128)(2,1)S(1)} async-done(((bf16[32,16,128]{2,1,0:T(8,128)(2,1)}), bf16[32,16,128]{2,1,0:T(8,128)(2,1)S(1)}, u32[]{:S(2)}, u32[]{:S(2)}) %all-to-all-start) | async-done | bytes 131104 | tf_op jit(solution)/shard_map/all_to_all | solution.py:127
  17.6 1.1 %middle.1 = bf16[32,16,128]{2,1,0:T(8,128)(2,1)} custom-call(bf16[32,16,128]{2,1,0:T(8,128)(2,1)S(1)} %all-to-all-done.bias_ref, f32[4,4,128,128]{3,2,1,0:T(8,128)S(1)} %get-tuple-element.10.e_ref, f32[4,4,128,128]{3,2,1,0:T(8,128)S(1)} %get-tuple-element.11.f_ref, f32[4,128,128]{2,1,0:T(8,128)S(1)} %get-tuple-element.15.a_ref), custom_call_target="tpu_custom_call" | custom-call | flops 1048576 | bytes 1048576 | tf_op jit(solution)/shard_map/middle/pallas_call | solution.py:135
  18.6 0.0 copy-start.4
  18.6 2.7 %all-to-all-start.1 = ((bf16[32,16,128]{2,1,0:T(8,128)(2,1)}), bf16[32,16,128]{2,1,0:T(8,128)(2,1)S(1)}, u32[]{:S(2)}, u32[]{:S(2)}) async-start(bf16[32,16,128]{2,1,0:T(8,128)(2,1)} %middle.1), calls=%async_computation.1 | async-start | bytes 262144 | tf_op jit(solution)/shard_map/all_to_all | solution.py:138
  21.3 0.0 copy-done.4
  21.3 1.7 %after.1 = (bf16[4,128,128]{2,1,0:T(8,128)(2,1)}, bf16[4,128,128]{2,1,0:T(8,128)(2,1)}, bf16[4,128,128]{2,1,0:T(8,128)(2,1)}) custom-call(bf16[32,16,128]{2,1,0:T(8,128)(2,1)S(1)} %all-to-all-done.bias_ref, f32[4,4,128,128]{3,2,1,0:T(8,128)S(1)} %get-tuple-element.10.e_ref, f32[4,4,128,128]{3,2,1,0:T(8,128)S(1)} %get-tuple-element.11.f_ref, ...), custom_call_target="tpu_custom_call" | custom-call | flops 1073741824 | bytes 1048576 | tf_op jit(solution)/shard_map/after/pallas_call | solution.py:140
  23.0 6.5 %all-to-all-done.1 = bf16[32,16,128]{2,1,0:T(8,128)(2,1)S(1)} async-done(((bf16[32,16,128]{2,1,0:T(8,128)(2,1)}), bf16[32,16,128]{2,1,0:T(8,128)(2,1)S(1)}, u32[]{:S(2)}, u32[]{:S(2)}) %all-to-all-start.1) | async-done | bytes 131104 | tf_op jit(solution)/shard_map/all_to_all | solution.py:138
  29.5 0.6 %convert_reduce_fusion = f32[16,128]{1,0:T(8,128)} fusion(bf16[32,16,128]{2,1,0:T(8,128)(2,1)S(1)} %all-to-all-done.1), kind=kLoop, calls=%fused_computation | loop fusion | flops 129024 | bytes 139264 | tf_op jit(solution)/shard_map/reduce_sum | solution.py:147
Async XLA Ops:
  0.6 8.7 %copy-start.2 = (bf16[4,128,128]{2,1,0:T(8,128)(2,1)S(1)}, bf16[4,128,128]{2,1,0:T(8,128)(2,1)}, u32[]{:S(2)}) copy-start(bf16[4,128,128]{2,1,0:T(8,128)(2,1)} %k_ref.3) | copy-start | bytes 393220
  2.0 7.3 %copy-start = (bf16[4,128,128]{2,1,0:T(8,128)(2,1)S(1)}, bf16[4,128,128]{2,1,0:T(8,128)(2,1)}, u32[]{:S(2)}) copy-start(bf16[4,128,128]{2,1,0:T(8,128)(2,1)} %v_ref.1) | copy-start | bytes 393220
  2.0 7.4 %copy-start.1 = (bf16[4,128,128]{2,1,0:T(8,128)(2,1)S(1)}, bf16[4,128,128]{2,1,0:T(8,128)(2,1)}, u32[]{:S(2)}) copy-start(bf16[4,128,128]{2,1,0:T(8,128)(2,1)} %q_ref.3) | copy-start | bytes 393220
  2.0 15.5 %all-to-all-start = ((bf16[32,16,128]{2,1,0:T(8,128)(2,1)}), bf16[32,16,128]{2,1,0:T(8,128)(2,1)S(1)}, u32[]{:S(2)}, u32[]{:S(2)}) async-start(bf16[32,16,128]{2,1,0:T(8,128)(2,1)} %broadcast_in_dim.8), calls=%async_computation | async-start | bytes 262144 | tf_op jit(solution)/shard_map/all_to_all | solution.py:127
  9.4 0.9 %copy-start.3 = (bf16[4,128,128]{2,1,0:T(8,128)(2,1)S(1)}, bf16[4,128,128]{2,1,0:T(8,128)(2,1)}, u32[]{:S(2)}) copy-start(bf16[4,128,128]{2,1,0:T(8,128)(2,1)} %g_ref.3) | copy-start | bytes 393220
  10.3 0.7 %copy-start.5 = (f32[4,4,128]{2,1,0:T(4,128)S(1)}, f32[4,4,128]{2,1,0:T(4,128)}, u32[]{:S(2)}) copy-start(f32[4,4,128]{2,1,0:T(4,128)} %param.10) | copy-start | bytes 24580
  18.6 2.7 %copy-start.4 = (bf16[4,128,128]{2,1,0:T(8,128)(2,1)S(1)}, bf16[4,128,128]{2,1,0:T(8,128)(2,1)}, u32[]{:S(2)}) copy-start(bf16[4,128,128]{2,1,0:T(8,128)(2,1)} %g_ref.3) | copy-start | bytes 393220
  18.6 10.9 %all-to-all-start.1 = ((bf16[32,16,128]{2,1,0:T(8,128)(2,1)}), bf16[32,16,128]{2,1,0:T(8,128)(2,1)S(1)}, u32[]{:S(2)}, u32[]{:S(2)}) async-start(bf16[32,16,128]{2,1,0:T(8,128)(2,1)} %middle.1), calls=%async_computation.1 | async-start | bytes 262144 | tf_op jit(solution)/shard_map/all_to_all | solution.py:138

commit v3 on v1

v3 whole, which is shorter than its diff:
```python
import functools
import math

import jax
import jax.numpy as jnp
from jax import lax
from jax.experimental import pallas as pl
from jax.experimental.pallas import tpu as pltpu
from jax.sharding import PartitionSpec as P

NN = (((1,), (0,)), ((), ()))
NT = (((1,), (1,)), ((), ()))
LANES = 128
LOG2E = math.log2(math.e)


def product(left, right, form=NN):
    return lax.dot_general(left, right, form, preferred_element_type=jnp.float32)


def head_lanes(shape, head, width):
    lane = lax.broadcasted_iota(jnp.int32, shape, len(shape) - 1)
    return (lane >= head * width) & (lane < (head + 1) * width)


def only_head(array, head, width):
    return jnp.where(head_lanes(array.shape, head, width), array, jnp.zeros_like(array))


def spread_rows(spread_ref, array):
    for piece in range(array.shape[1] // LANES):
        spread_ref[piece] = array[:, piece * LANES : (piece + 1) * LANES]


def head_rows(spread_ref, head, heads, length):
    here = pl.ds(head, length, stride=heads)
    pieces = [spread_ref[piece, here, :] for piece in range(spread_ref.shape[0])]
    return pieces[0] if len(pieces) == 1 else jnp.concatenate(pieces, axis=1)


def keep_head_rows(spread_ref, head, heads, array):
    length = array.shape[0]
    for piece in range(spread_ref.shape[0]):
        lanes = array[:, piece * LANES : (piece + 1) * LANES]
        spread_ref[piece, pl.ds(head, length, stride=heads), :] = lanes


def load_kernel(bias_hbm, norm_hbm, g_hbm, copies_ref, norm_ref, g_ref, bias_ref, sems):
    pairs = ((bias_hbm, bias_ref), (norm_hbm, norm_ref), (g_hbm, g_ref))
    moves = [pltpu.make_async_copy(a, b, sems.at[n]) for n, (a, b) in enumerate(pairs)]
    for move in moves:
        move.start()
    moves[0].wait()
    copies_ref[...] = jnp.broadcast_to(bias_ref[...][None], copies_ref.shape)
    for move in moves[1:]:
        move.wait()


def store_kernel(
    received_ref, dq_ref, dk_ref, dv_ref, sum_hbm, dq_hbm, dk_hbm, dv_hbm, sum_ref, sems
):
    pairs = ((dq_ref, dq_hbm), (dk_ref, dk_hbm), (dv_ref, dv_hbm), (sum_ref, sum_hbm))
    moves = [pltpu.make_async_copy(a, b, sems.at[n]) for n, (a, b) in enumerate(pairs)]
    for move in moves[:3]:
        move.start()
    sum_ref[...] = jnp.sum(received_ref[...].astype(jnp.float32), axis=0)
    moves[3].start()
    for move in moves:
        move.wait()


def attend_kernel(
    heads, bias_ref, q_ref, k_ref, v_ref, g_ref, norm_ref,
    part_ref, dq_ref, dk_ref, dv_ref, spread_ref,
):
    rows, length, channels = q_ref.shape
    width = channels // heads
    scale = width ** (-0.5)
    low = jnp.bfloat16
    every = range(heads)
    bias = bias_ref[...].reshape(heads * length, length).astype(jnp.float32) * LOG2E
    spread_rows(spread_ref, bias)
    logits = [head_rows(spread_ref, head, heads, length) for head in every]
    norms = jnp.transpose(norm_ref[...]) * LOG2E

    def stack(array):
        return jnp.concatenate([only_head(array, head, width) for head in every], 0)

    def turned_stack(array):
        turned = jnp.transpose(array)
        line = lax.broadcasted_iota(jnp.int32, turned.shape, 0)
        zero = jnp.zeros_like(turned)
        kept = [(line >= h * width) & (line < (h + 1) * width) for h in every]
        return jnp.concatenate([jnp.where(mask, turned, zero) for mask in kept], 1)

    sums = [None] * heads
    for row in range(rows):
        q, k, v, g = q_ref[row], k_ref[row], v_ref[row], g_ref[row]
        s_all, p_all = product(stack(q), k, NT), product(stack(g), v, NT)
        w_low, s_low = [], []
        for head in every:
            column = row * heads + head
            weights = jnp.exp2(
                s_all[head * length : (head + 1) * length] * (scale * LOG2E) + (logits[head] - norms[:, column : column + 1])
            )
            slopes = p_all[head * length : (head + 1) * length]
            centre = jnp.sum(weights * slopes, axis=1, keepdims=True)
            grads = weights * (slopes - centre)
            sums[head] = grads if row == 0 else sums[head] + grads
            w_low.append(weights.astype(low))
            s_low.append(grads.astype(low))
        dq = product(jnp.concatenate(s_low, 1), stack(k))
        dkt = product(turned_stack(q), jnp.concatenate(s_low, 0))
        dvt = product(turned_stack(g), jnp.concatenate(w_low, 0))
        dq_ref[row] = (dq * scale).astype(low)
        dk_ref[row] = jnp.transpose((dkt * scale).astype(low))
        dv_ref[row] = jnp.transpose(dvt.astype(low))
    for head in every:
        keep_head_rows(spread_ref, head, heads, sums[head])
    for piece in range(length // LANES):
        lanes = spread_ref[piece].astype(low).reshape(part_ref.shape[:2] + (LANES,))
        part_ref[:, :, piece * LANES : (piece + 1) * LANES] = lanes


def call(kernel, name, outputs, scratch=(), ins=None, outs=None):
    def place(space):
        return pl.BlockSpec(memory_space=space)

    specs = {}
    if ins is not None:
        specs["in_specs"] = [place(space) for space in ins]
    if outs is not None:
        specs["out_specs"] = tuple(place(space) for space in outs)
    return pl.pallas_call(
        kernel,
        name=name,
        out_shape=outputs,
        scratch_shapes=scratch,
        compiler_params=pltpu.CompilerParams(vmem_limit_bytes=24 << 20),
        **specs,
    )


def local(queries, keys, values, grads_out, log_norm, bias):
    heads = bias.shape[1]
    rows, length, channels = queries.shape
    devices = lax.axis_size("row")
    shape, f32, bf16 = jax.ShapeDtypeStruct, jnp.float32, jnp.bfloat16
    hbm, vmem, dma = pltpu.HBM, pltpu.VMEM, pltpu.SemaphoreType.DMA
    block = (rows * heads, length)
    exchanged = shape((devices,) + block, bf16)
    pair = shape(queries.shape, bf16)
    copies, norms, cotangents = call(
        load_kernel,
        "load",
        (exchanged, shape(block, f32), pair),
        (vmem(block, bf16), dma((3,))),
        (hbm,) * 3,
        (vmem,) * 3,
    )(*(pltpu.with_memory_space_constraint(array, hbm) for array in (bias.reshape(block), log_norm.reshape(block), grads_out)))
    gathered = lax.all_to_all(copies, "row", 0, 0)
    wide = vmem((length // LANES, length * heads, LANES), f32)
    part, *grads = call(
        functools.partial(attend_kernel, heads), "attend", (exchanged,) + (pair,) * 3, (wide,)
    )(gathered, queries, keys, values, cotangents, norms)
    received = lax.all_to_all(part, "row", 0, 0)
    bias_grad, *grads = call(
        store_kernel,
        "store",
        (shape(block, f32),) + (pair,) * 3,
        (vmem(block, f32), dma((4,))),
        (vmem,) * 4,
        (hbm,) * 4,
    )(received, *grads)
    return (*grads, bias_grad.reshape(bias.shape))


def solution(mesh):
    placed = P(("crop", "row"), None, None)
    return jax.shard_map(
        local, mesh=mesh, in_specs=(placed,) * 6, out_specs=(placed,) * 4, check_vma=False
    )
```

time: 34 us -> 29.8 us (0.88)
  blocking collectives: 0 us -> 25.3 us
  waiting for transfers between devices: 12 us -> 0 us
  starting transfers between devices: 9.89 us -> 0 us
  local copies, waits for them, and re-layouts: 8.84 us -> 0.02 us
  Pallas kernels: 0 us -> 3.58 us
  matrix products: 1.86 us -> 0 us
    all_to_all x0 -> x2, blocking collectives: none -> 25.3 us  [the longest x1 15.3 us: local(): gathered = lax.all_to_all(copies, 'row', 0, 0)]
    all_to_all x2 -> x0, waiting for transfers between devices: 12 us -> none  [the longest x1 7.04 us: scatter_sum(): received = lax.all_to_all(parts, 'row', 0, 0)]
    all_to_all x2 -> x0, starting transfers between devices: 9.89 us -> none  [the longest x1 7.33 us: gather_rows(): return lax.all_to_all(copies, 'row', 0, 0)]
    unnamed x19 -> x6, local copies, waits for them, and re-layouts: 7.01 us -> 0.02 us
    pallas_call x0 -> x3, Pallas kernels: none -> 3.58 us  [the longest x1 1.8 us: local(): call(functools.partial(attend_kernel, heads), 'attend', (exchanged,) + (p...]
    dot_general x5 -> x0, matrix products: 1.86 us -> none  [product(): return jnp.einsum(form, left, right, preferred_element_type=jnp.float32)]
    reshape x1 -> x0, local copies, waits for them, and re-layouts: 0.7 us -> none  [scatter_sum(): partial.astype(jnp.bfloat16).reshape((devices, rows) + partial.shape[1:])]
    broadcast_in_dim x1 -> x0, local copies, waits for them, and re-layouts: 0.69 us -> none  [gather_rows(): copies = jnp.broadcast_to(block[None], (devices,) + block.shape)]
  transfers between devices with their start and end apart: 2 -> 0, of which waited for: 2 -> 0; matrix products, arithmetic and copies ran while one was open for 6% -> 0% of each run, Pallas kernels for 0% -> 0%
where the time goes in v3:
time: 29.8 us; the launch traced here: 29.6 us
  blocking collectives  25.3 us (85%)
  Pallas kernels  3.58 us (12%)
  between operations  0.68 us (2%)
    all_to_all x1, blocking collectives, local(): gathered = lax.all_to_all(copies, 'row', 0, 0)  15.3 us
    all_to_all x1, blocking collectives, local(): received = lax.all_to_all(part, 'row', 0, 0)  9.97 us
    pallas_call x1, Pallas kernels, local(): call(functools.partial(attend_kernel, heads), 'attend', (exchanged,) + (p...  1.8 us
    pallas_call x1, Pallas kernels, local(): call(load_kernel, 'load', (exchanged, shape(block, f32), pair), (vmem(blo...  1 us
    pallas_call x1, Pallas kernels, local(): call(store_kernel, 'store', (shape(block, f32),) + (pair,) * 3, (vmem(blo...  0.78 us

profile of v3, /device:TPU:0, one launch (start us, length us, event | category | flops | bytes accessed | tf_op | source)
XLA Modules:
  0.0 29.6 jit_solution(1604286953954404649)
XLA Ops:
  0.6 0.0 copy-start.2
  0.6 1.0 %load.1 = (bf16[32,16,128]{2,1,0:T(8,128)(2,1)S(1)}, f32[16,128]{1,0:T(8,128)S(1)}, bf16[4,128,128]{2,1,0:T(8,128)(2,1)S(1)}) custom-call(bf16[16,128]{1,0:T(8,128)(2,1)} %bitcast.4, f32[16,128]{1,0:T(8,128)} %bitcast.3, bf16[4,128,128]{2,1,0:T(8,128)(2,1)} %g_hbm.1), custom_call_target="tpu_custom_call" | custom-call | tf_op jit(solution)/shard_map/load/pallas_call | solution.py:153
  1.6 0.0 copy-start
  1.7 0.0 copy-start.1
  1.7 15.3 %all_to_all.10.bias_ref = bf16[32,16,128]{2,1,0:T(8,128)(2,1)S(1)} all-to-all(bf16[32,16,128]{2,1,0:T(8,128)(2,1)S(1)} %get-tuple-element.15), channel_id=1, replica_groups=mesh['crop'=1,'row'=32] {'row'}, dimensions={0} | all-to-all | bytes 262144 | tf_op jit(solution)/shard_map/all_to_all | solution.py:161
  17.0 0.0 copy-done.2
  17.0 0.0 copy-done
  17.0 0.0 copy-done.1
  17.0 1.8 %attend.1 = (bf16[32,16,128]{2,1,0:T(8,128)(2,1)S(1)}, bf16[4,128,128]{2,1,0:T(8,128)(2,1)S(1)}, bf16[4,128,128]{2,1,0:T(8,128)(2,1)S(1)}, bf16[4,128,128]{2,1,0:T(8,128)(2,1)S(1)}) custom-call(bf16[32,16,128]{2,1,0:T(8,128)(2,1)S(1)} %all_to_all.10.bias_ref, bf16[4,128,128]{2,1,0:T(8,128)(2,1)S(1)} %copy-done, bf16[4,128,128]{2,1,0:T(8,128)(2,1)S(1)} %copy-done.1, ...), custom_call_target="tpu_custom_call" | custom-call | tf_op jit(solution)/shard_map/attend/pallas_call | solution.py:163
  18.8 10.0 %all_to_all.11.received_ref = bf16[32,16,128]{2,1,0:T(8,128)(2,1)S(1)} all-to-all(bf16[32,16,128]{2,1,0:T(8,128)(2,1)S(1)} %get-tuple-element.18), channel_id=1, replica_groups=mesh['crop'=1,'row'=32] {'row'}, dimensions={0} | all-to-all | bytes 262144 | tf_op jit(solution)/shard_map/all_to_all | solution.py:166
  28.8 0.8 %store.1 = (f32[16,128]{1,0:T(8,128)}, bf16[4,128,128]{2,1,0:T(8,128)(2,1)}, bf16[4,128,128]{2,1,0:T(8,128)(2,1)}, bf16[4,128,128]{2,1,0:T(8,128)(2,1)}) custom-call(bf16[32,16,128]{2,1,0:T(8,128)(2,1)S(1)} %all_to_all.11.received_ref, bf16[4,128,128]{2,1,0:T(8,128)(2,1)S(1)} %get-tuple-element.19.dq_ref, bf16[4,128,128]{2,1,0:T(8,128)(2,1)S(1)} %get-tuple-element.20.dk_ref, ...), custom_call_target="tpu_custom_call" | custom-call | tf_op jit(solution)/shard_map/store/pallas_call | solution.py:167
Async XLA Ops:
  0.6 16.4 %copy-start.2 = (bf16[4,128,128]{2,1,0:T(8,128)(2,1)S(1)}, bf16[4,128,128]{2,1,0:T(8,128)(2,1)}, u32[]{:S(2)}) copy-start(bf16[4,128,128]{2,1,0:T(8,128)(2,1)} %v_ref.1) | copy-start | bytes 393220
  1.6 15.4 %copy-start = (bf16[4,128,128]{2,1,0:T(8,128)(2,1)S(1)}, bf16[4,128,128]{2,1,0:T(8,128)(2,1)}, u32[]{:S(2)}) copy-start(bf16[4,128,128]{2,1,0:T(8,128)(2,1)} %q_ref.1) | copy-start | bytes 393220
  1.7 15.4 %copy-start.1 = (bf16[4,128,128]{2,1,0:T(8,128)(2,1)S(1)}, bf16[4,128,128]{2,1,0:T(8,128)(2,1)}, u32[]{:S(2)}) copy-start(bf16[4,128,128]{2,1,0:T(8,128)(2,1)} %k_ref.1) | copy-start | bytes 393220

commit v4 on v3

--- a/solution.py
+++ b/solution.py
@@ -1,5 +1,4 @@
 import functools
-import math
 
 import jax
 import jax.numpy as jnp
@@ -11,7 +10,6 @@
 NN = (((1,), (0,)), ((), ()))
 NT = (((1,), (1,)), ((), ()))
 LANES = 128
-LOG2E = math.log2(math.e)
 
 
 def product(left, right, form=NN):
@@ -46,7 +44,8 @@
 
 
 def load_kernel(bias_hbm, norm_hbm, g_hbm, copies_ref, norm_ref, g_ref, bias_ref, sems):
-    pairs = ((bias_hbm, bias_ref), (norm_hbm, norm_ref), (g_hbm, g_ref))
+    pairs = [(bias_hbm, bias_ref), (norm_hbm, norm_ref)]
+    pairs += [(g_hbm.at[row], g_ref.at[row]) for row in range(g_ref.shape[0])]
     moves = [pltpu.make_async_copy(a, b, sems.at[n]) for n, (a, b) in enumerate(pairs)]
     for move in moves:
         move.start()
@@ -69,6 +68,18 @@
         move.wait()
 
 
+def identity(length, dtype):
+    rows = lax.broadcasted_iota(jnp.int32, (length, length), 0)
+    columns = lax.broadcasted_iota(jnp.int32, (length, length), 1)
+    return jnp.where(rows == columns, 1.0, 0.0).astype(dtype)
+
+
+def joined(parts, width):
+    total = parts[0]
+    for head in range(1, len(parts)):
+        total = jnp.where(head_lanes(total.shape, head, width), parts[head], total)
+    return total
+
 def attend_kernel(
     heads, bias_ref, q_ref, k_ref, v_ref, g_ref, norm_ref,
     part_ref, dq_ref, dk_ref, dv_ref, spread_ref,
@@ -78,45 +89,57 @@
     scale = width ** (-0.5)
     low = jnp.bfloat16
     every = range(heads)
-    bias = bias_ref[...].reshape(heads * length, length).astype(jnp.float32) * LOG2E
-    spread_rows(spread_ref, bias)
-    logits = [head_rows(spread_ref, head, heads, length) for head in every]
-    norms = jnp.transpose(norm_ref[...]) * LOG2E
+    eye = identity(length, low)
 
     def stack(array):
         return jnp.concatenate([only_head(array, head, width) for head in every], 0)
 
-    def turned_stack(array):
-        turned = jnp.transpose(array)
-        line = lax.broadcasted_iota(jnp.int32, turned.shape, 0)
-        zero = jnp.zeros_like(turned)
-        kept = [(line >= h * width) & (line < (h + 1) * width) for h in every]
-        return jnp.concatenate([jnp.where(mask, turned, zero) for mask in kept], 1)
-
+    def cut(array, head):
+        return array[head * length : (head + 1) * length]
+
+    def mine(array, head):
+        return array[head * width : (head + 1) * width]
+
+    spread_rows(spread_ref, bias_ref[...].reshape(heads * length, length).astype(jnp.float32))
+    rows_of = [head_rows(spread_ref, head, heads, length).astype(low) for head in every]
+    logits = [product(eye, rows_of[head], NT) for head in every]
+    norms = norm_ref[...]
     sums = [None] * heads
+
+    def scored(row):
+        return (
+            product(stack(k_ref[row]), q_ref[row], NT),
+            product(stack(v_ref[row]), g_ref[row], NT),
+        )
+
+    ahead = scored(0)
     for row in range(rows):
         q, k, v, g = q_ref[row], k_ref[row], v_ref[row], g_ref[row]
-        s_all, p_all = product(stack(q), k, NT), product(stack(g), v, NT)
+        s_all, p_all = ahead
+        if row + 1 < rows:
+            ahead = scored(row + 1)
+        kt = jnp.transpose(k)
         w_low, s_low = [], []
         for head in every:
-            column = row * heads + head
-            weights = jnp.exp2(
-                s_all[head * length : (head + 1) * length] * (scale * LOG2E) + (logits[head] - norms[:, column : column + 1])
+            line = row * heads + head
+            weights = jnp.exp(
+                cut(s_all, head) * scale + (logits[head] - norms[line : line + 1])
             )
-            slopes = p_all[head * length : (head + 1) * length]
-            centre = jnp.sum(weights * slopes, axis=1, keepdims=True)
+            slopes = cut(p_all, head)
+            centre = jnp.sum(weights * slopes, axis=0, keepdims=True)
             grads = weights * (slopes - centre)
             sums[head] = grads if row == 0 else sums[head] + grads
+            if row == rows - 1:
+                upright = jnp.transpose(sums[head].astype(low)).astype(jnp.float32)
+                keep_head_rows(spread_ref, head, heads, upright)
             w_low.append(weights.astype(low))
             s_low.append(grads.astype(low))
-        dq = product(jnp.concatenate(s_low, 1), stack(k))
-        dkt = product(turned_stack(q), jnp.concatenate(s_low, 0))
-        dvt = product(turned_stack(g), jnp.concatenate(w_low, 0))
-        dq_ref[row] = (dq * scale).astype(low)
-        dk_ref[row] = jnp.transpose((dkt * scale).astype(low))
-        dv_ref[row] = jnp.transpose(dvt.astype(low))
-    for head in every:
-        keep_head_rows(spread_ref, head, heads, sums[head])
+        dk = product(jnp.concatenate(s_low, 0), q)
+        dv = product(jnp.concatenate(w_low, 0), g)
+        dqt = jnp.concatenate([product(mine(kt, h), s_low[h]) for h in every], 0)
+        dk_ref[row] = (joined([cut(dk, h) for h in every], width) * scale).astype(low)
+        dv_ref[row] = joined([cut(dv, h) for h in every], width).astype(low)
+        dq_ref[row] = jnp.transpose((dqt * scale).astype(low))
     for piece in range(length // LANES):
         lanes = spread_ref[piece].astype(low).reshape(part_ref.shape[:2] + (LANES,))
         part_ref[:, :, piece * LANES : (piece + 1) * LANES] = lanes
@@ -146,6 +169,7 @@
     rows, length, channels = queries.shape
     devices = lax.axis_size("row")
     shape, f32, bf16 = jax.ShapeDtypeStruct, jnp.float32, jnp.bfloat16
+    held = pltpu.with_memory_space_constraint
     hbm, vmem, dma = pltpu.HBM, pltpu.VMEM, pltpu.SemaphoreType.DMA
     block = (rows * heads, length)
     exchanged = shape((devices,) + block, bf16)
@@ -154,10 +178,10 @@
         load_kernel,
         "load",
         (exchanged, shape(block, f32), pair),
-        (vmem(block, bf16), dma((3,))),
+        (vmem(block, bf16), dma((2 + rows,))),
         (hbm,) * 3,
         (vmem,) * 3,
-    )(*(pltpu.with_memory_space_constraint(array, hbm) for array in (bias.reshape(block), log_norm.reshape(block), grads_out)))
+    )(*(held(array, hbm) for array in (bias.reshape(block), log_norm.reshape(block), grads_out)))
     gathered = lax.all_to_all(copies, "row", 0, 0)
     wide = vmem((length // LANES, length * heads, LANES), f32)
     part, *grads = call(

time: 29.8 us -> 29 us (0.973)
  Pallas kernels: 3.58 us -> 2.87 us
    pallas_call x1, Pallas kernels: 1.8 us -> 1.16 us  [local(): call(functools.partial(attend_kernel, heads), 'attend', (exchanged,) + (p...]
where the time goes in v4:
time: 29 us; the launch traced here: 28.9 us
  blocking collectives  25.3 us (87%)
  Pallas kernels  2.87 us (10%)
  between operations  0.68 us (2%)
    all_to_all x1, blocking collectives, local(): gathered = lax.all_to_all(copies, 'row', 0, 0)  15.3 us
    all_to_all x1, blocking collectives, local(): received = lax.all_to_all(part, 'row', 0, 0)  9.97 us
    pallas_call x1, Pallas kernels, local(): call(functools.partial(attend_kernel, heads), 'attend', (exchanged,) + (p...  1.16 us
    pallas_call x1, Pallas kernels, local(): call(load_kernel, 'load', (exchanged, shape(block, f32), pair), (vmem(blo...  0.93 us
    pallas_call x1, Pallas kernels, local(): call(store_kernel, 'store', (shape(block, f32),) + (pair,) * 3, (vmem(blo...  0.78 us

profile of v4, /device:TPU:0, one launch (start us, length us, event | category | flops | bytes accessed | tf_op | source)
XLA Modules:
  0.0 28.9 jit_solution(14667125571481106138)
XLA Ops:
  0.6 0.0 copy-start.2
  0.6 0.9 %load.1 = (bf16[32,16,128]{2,1,0:T(8,128)(2,1)S(1)}, f32[16,128]{1,0:T(8,128)S(1)}, bf16[4,128,128]{2,1,0:T(8,128)(2,1)S(1)}) custom-call(bf16[16,128]{1,0:T(8,128)(2,1)} %bitcast.4, f32[16,128]{1,0:T(8,128)} %bitcast.3, bf16[4,128,128]{2,1,0:T(8,128)(2,1)} %g_hbm.1), custom_call_target="tpu_custom_call" | custom-call | tf_op jit(solution)/shard_map/load/pallas_call | solution.py:177
  1.6 0.0 copy-start
  1.6 0.0 copy-start.1
  1.6 15.3 %all_to_all.10.bias_ref = bf16[32,16,128]{2,1,0:T(8,128)(2,1)S(1)} all-to-all(bf16[32,16,128]{2,1,0:T(8,128)(2,1)S(1)} %get-tuple-element.15), channel_id=1, replica_groups=mesh['crop'=1,'row'=32] {'row'}, dimensions={0} | all-to-all | bytes 262144 | tf_op jit(solution)/shard_map/all_to_all | solution.py:185
  16.9 0.0 copy-done.2
  16.9 0.0 copy-done
  16.9 0.0 copy-done.1
  16.9 1.2 %attend.1 = (bf16[32,16,128]{2,1,0:T(8,128)(2,1)S(1)}, bf16[4,128,128]{2,1,0:T(8,128)(2,1)S(1)}, bf16[4,128,128]{2,1,0:T(8,128)(2,1)S(1)}, bf16[4,128,128]{2,1,0:T(8,128)(2,1)S(1)}) custom-call(bf16[32,16,128]{2,1,0:T(8,128)(2,1)S(1)} %all_to_all.10.bias_ref, bf16[4,128,128]{2,1,0:T(8,128)(2,1)S(1)} %copy-done, bf16[4,128,128]{2,1,0:T(8,128)(2,1)S(1)} %copy-done.1, ...), custom_call_target="tpu_custom_call" | custom-call | tf_op jit(solution)/shard_map/attend/pallas_call | solution.py:187
  18.1 10.0 %all_to_all.11.received_ref = bf16[32,16,128]{2,1,0:T(8,128)(2,1)S(1)} all-to-all(bf16[32,16,128]{2,1,0:T(8,128)(2,1)S(1)} %get-tuple-element.18), channel_id=1, replica_groups=mesh['crop'=1,'row'=32] {'row'}, dimensions={0} | all-to-all | bytes 262144 | tf_op jit(solution)/shard_map/all_to_all | solution.py:190
  28.1 0.8 %store.1 = (f32[16,128]{1,0:T(8,128)}, bf16[4,128,128]{2,1,0:T(8,128)(2,1)}, bf16[4,128,128]{2,1,0:T(8,128)(2,1)}, bf16[4,128,128]{2,1,0:T(8,128)(2,1)}) custom-call(bf16[32,16,128]{2,1,0:T(8,128)(2,1)S(1)} %all_to_all.11.received_ref, bf16[4,128,128]{2,1,0:T(8,128)(2,1)S(1)} %get-tuple-element.19.dq_ref, bf16[4,128,128]{2,1,0:T(8,128)(2,1)S(1)} %get-tuple-element.20.dk_ref, ...), custom_call_target="tpu_custom_call" | custom-call | tf_op jit(solution)/shard_map/store/pallas_call | solution.py:191
Async XLA Ops:
  0.6 16.3 %copy-start.2 = (bf16[4,128,128]{2,1,0:T(8,128)(2,1)S(1)}, bf16[4,128,128]{2,1,0:T(8,128)(2,1)}, u32[]{:S(2)}) copy-start(bf16[4,128,128]{2,1,0:T(8,128)(2,1)} %v_ref.1) | copy-start | bytes 393220
  1.6 15.4 %copy-start = (bf16[4,128,128]{2,1,0:T(8,128)(2,1)S(1)}, bf16[4,128,128]{2,1,0:T(8,128)(2,1)}, u32[]{:S(2)}) copy-start(bf16[4,128,128]{2,1,0:T(8,128)(2,1)} %q_ref.1) | copy-start | bytes 393220
  1.6 15.4 %copy-start.1 = (bf16[4,128,128]{2,1,0:T(8,128)(2,1)S(1)}, bf16[4,128,128]{2,1,0:T(8,128)(2,1)}, u32[]{:S(2)}) copy-start(bf16[4,128,128]{2,1,0:T(8,128)(2,1)} %k_ref.1) | copy-start | bytes 393220

commit v5 on v4

--- a/solution.py
+++ b/solution.py
@@ -43,16 +43,8 @@
         spread_ref[piece, pl.ds(head, length, stride=heads), :] = lanes
 
 
-def load_kernel(bias_hbm, norm_hbm, g_hbm, copies_ref, norm_ref, g_ref, bias_ref, sems):
-    pairs = [(bias_hbm, bias_ref), (norm_hbm, norm_ref)]
-    pairs += [(g_hbm.at[row], g_ref.at[row]) for row in range(g_ref.shape[0])]
-    moves = [pltpu.make_async_copy(a, b, sems.at[n]) for n, (a, b) in enumerate(pairs)]
-    for move in moves:
-        move.start()
-    moves[0].wait()
+def load_kernel(bias_ref, copies_ref):
     copies_ref[...] = jnp.broadcast_to(bias_ref[...][None], copies_ref.shape)
-    for move in moves[1:]:
-        move.wait()
 
 
 def store_kernel(
@@ -102,7 +94,8 @@
 
     spread_rows(spread_ref, bias_ref[...].reshape(heads * length, length).astype(jnp.float32))
     rows_of = [head_rows(spread_ref, head, heads, length).astype(low) for head in every]
-    logits = [product(eye, rows_of[head], NT) for head in every]
+    turned = product(eye, jnp.concatenate(rows_of, 0), NT)
+    logits = [turned[:, head * length : (head + 1) * length] for head in every]
     norms = norm_ref[...]
     sums = [None] * heads
 
@@ -145,7 +138,7 @@
         part_ref[:, :, piece * LANES : (piece + 1) * LANES] = lanes
 
 
-def call(kernel, name, outputs, scratch=(), ins=None, outs=None):
+def call(kernel, name, outputs, scratch=(), ins=None, outs=None, cost=None):
     def place(space):
         return pl.BlockSpec(memory_space=space)
 
@@ -157,6 +150,7 @@
     return pl.pallas_call(
         kernel,
         name=name,
+        cost_estimate=cost,
         out_shape=outputs,
         scratch_shapes=scratch,
         compiler_params=pltpu.CompilerParams(vmem_limit_bytes=24 << 20),
@@ -174,19 +168,12 @@
     block = (rows * heads, length)
     exchanged = shape((devices,) + block, bf16)
     pair = shape(queries.shape, bf16)
-    copies, norms, cotangents = call(
-        load_kernel,
-        "load",
-        (exchanged, shape(block, f32), pair),
-        (vmem(block, bf16), dma((2 + rows,))),
-        (hbm,) * 3,
-        (vmem,) * 3,
-    )(*(held(array, hbm) for array in (bias.reshape(block), log_norm.reshape(block), grads_out)))
+    copies = call(load_kernel, "load", exchanged, cost=pl.CostEstimate(flops=1 << 34, bytes_accessed=1 << 26, transcendentals=0))(bias.reshape(block))
     gathered = lax.all_to_all(copies, "row", 0, 0)
     wide = vmem((length // LANES, length * heads, LANES), f32)
     part, *grads = call(
         functools.partial(attend_kernel, heads), "attend", (exchanged,) + (pair,) * 3, (wide,)
-    )(gathered, queries, keys, values, cotangents, norms)
+    )(gathered, queries, keys, values, grads_out, log_norm.reshape(block))
     received = lax.all_to_all(part, "row", 0, 0)
     bias_grad, *grads = call(
         store_kernel,

time: 29 us -> 28.8 us (level)
  Pallas kernels: 2.87 us -> 1.9 us
  local copies, waits for them, and re-layouts: 0.02 us -> 0.7 us
    pallas_call x1, Pallas kernels: 0.93 us -> 0.02 us  [local(): call(load_kernel, 'load', exchanged, cost=pl.CostEstimate(flops=1 << 34,...]
    unnamed x6 -> x12, local copies, waits for them, and re-layouts: 0.02 us -> 0.7 us
where the time goes in v5:
time: 28.8 us; the launch traced here: 28.6 us
  blocking collectives  25.3 us (88%)
  Pallas kernels  1.9 us (7%)
  local copies, waits for them, and re-layouts  0.7 us (2%)
  between operations  0.69 us (2%)
    all_to_all x1, blocking collectives, local(): gathered = lax.all_to_all(copies, 'row', 0, 0)  15.3 us
    all_to_all x1, blocking collectives, local(): received = lax.all_to_all(part, 'row', 0, 0)  9.96 us
    pallas_call x1, Pallas kernels, local(): call(functools.partial(attend_kernel, heads), 'attend', (exchanged,) + (p...  1.1 us
    pallas_call x1, Pallas kernels, local(): call(store_kernel, 'store', (shape(block, f32),) + (pair,) * 3, (vmem(blo...  0.78 us
    unnamed x12, local copies, waits for them, and re-layouts  0.7 us

profile of v5, /device:TPU:0, one launch (start us, length us, event | category | flops | bytes accessed | tf_op | source)
XLA Modules:
  0.0 28.6 jit_solution(15910810802147464119)
XLA Ops:
  0.6 0.0 copy-start.5
  0.6 0.7 %copy-done.5 = bf16[4,4,128]{2,1,0:T(4,128)(2,1)S(1)} copy-done((bf16[4,4,128]{2,1,0:T(4,128)(2,1)S(1)}, bf16[4,4,128]{2,1,0:T(4,128)(2,1)}, u32[]{:S(2)}) %copy-start.5) | copy-done | bytes 4120
  1.3 0.0 copy-start.2
  1.3 0.0 copy-start.3
  1.3 0.0 copy-start.4
  1.3 0.0 copy-start
  1.4 0.0 copy-start.1
  1.4 15.3 %all_to_all.10.bias_ref = bf16[32,16,128]{2,1,0:T(8,128)(2,1)S(1)} all-to-all(bf16[32,16,128]{2,1,0:T(8,128)(2,1)S(1)} %load.1), channel_id=1, replica_groups=mesh['crop'=1,'row'=32] {'row'}, dimensions={0} | all-to-all | bytes 262144 | tf_op jit(solution)/shard_map/all_to_all | solution.py:172
  16.7 0.0 copy-done.2
  16.7 0.0 copy-done.3
  16.7 0.0 copy-done.4
  16.7 0.0 copy-done
  16.7 0.0 copy-done.1
  16.7 1.1 %attend.1 = (bf16[32,16,128]{2,1,0:T(8,128)(2,1)S(1)}, bf16[4,128,128]{2,1,0:T(8,128)(2,1)S(1)}, bf16[4,128,128]{2,1,0:T(8,128)(2,1)S(1)}, bf16[4,128,128]{2,1,0:T(8,128)(2,1)S(1)}) custom-call(bf16[32,16,128]{2,1,0:T(8,128)(2,1)S(1)} %all_to_all.10.bias_ref, bf16[4,128,128]{2,1,0:T(8,128)(2,1)S(1)} %copy-done, bf16[4,128,128]{2,1,0:T(8,128)(2,1)S(1)} %copy-done.1, ...), custom_call_target="tpu_custom_call" | custom-call | tf_op jit(solution)/shard_map/attend/pallas_call | solution.py:174
  17.8 10.0 %all_to_all.11.received_ref = bf16[32,16,128]{2,1,0:T(8,128)(2,1)S(1)} all-to-all(bf16[32,16,128]{2,1,0:T(8,128)(2,1)S(1)} %get-tuple-element.12), channel_id=1, replica_groups=mesh['crop'=1,'row'=32] {'row'}, dimensions={0} | all-to-all | bytes 262144 | tf_op jit(solution)/shard_map/all_to_all | solution.py:177
  27.8 0.8 %store.1 = (f32[16,128]{1,0:T(8,128)}, bf16[4,128,128]{2,1,0:T(8,128)(2,1)}, bf16[4,128,128]{2,1,0:T(8,128)(2,1)}, bf16[4,128,128]{2,1,0:T(8,128)(2,1)}) custom-call(bf16[32,16,128]{2,1,0:T(8,128)(2,1)S(1)} %all_to_all.11.received_ref, bf16[4,128,128]{2,1,0:T(8,128)(2,1)S(1)} %get-tuple-element.13.dq_ref, bf16[4,128,128]{2,1,0:T(8,128)(2,1)S(1)} %get-tuple-element.14.dk_ref, ...), custom_call_target="tpu_custom_call" | custom-call | tf_op jit(solution)/shard_map/store/pallas_call | solution.py:178
  (1 shorter events, 0.0 us)
Async XLA Ops:
  0.6 0.7 %copy-start.5 = (bf16[4,4,128]{2,1,0:T(4,128)(2,1)S(1)}, bf16[4,4,128]{2,1,0:T(4,128)(2,1)}, u32[]{:S(2)}) copy-start(bf16[4,4,128]{2,1,0:T(4,128)(2,1)} %param.11) | copy-start | bytes 12292
  1.3 15.4 %copy-start.2 = (bf16[4,128,128]{2,1,0:T(8,128)(2,1)S(1)}, bf16[4,128,128]{2,1,0:T(8,128)(2,1)}, u32[]{:S(2)}) copy-start(bf16[4,128,128]{2,1,0:T(8,128)(2,1)} %v_ref.1) | copy-start | bytes 393220
  1.3 15.4 %copy-start.3 = (bf16[4,128,128]{2,1,0:T(8,128)(2,1)S(1)}, bf16[4,128,128]{2,1,0:T(8,128)(2,1)}, u32[]{:S(2)}) copy-start(bf16[4,128,128]{2,1,0:T(8,128)(2,1)} %g_ref.1) | copy-start | bytes 393220
  1.3 15.4 %copy-start.4 = (f32[4,4,128]{2,1,0:T(4,128)S(1)}, f32[4,4,128]{2,1,0:T(4,128)}, u32[]{:S(2)}) copy-start(f32[4,4,128]{2,1,0:T(4,128)} %param.10) | copy-start | bytes 24580
  1.3 15.4 %copy-start = (bf16[4,128,128]{2,1,0:T(8,128)(2,1)S(1)}, bf16[4,128,128]{2,1,0:T(8,128)(2,1)}, u32[]{:S(2)}) copy-start(bf16[4,128,128]{2,1,0:T(8,128)(2,1)} %q_ref.1) | copy-start | bytes 393220
  1.4 15.4 %copy-start.1 = (bf16[4,128,128]{2,1,0:T(8,128)(2,1)S(1)}, bf16[4,128,128]{2,1,0:T(8,128)(2,1)}, u32[]{:S(2)}) copy-start(bf16[4,128,128]{2,1,0:T(8,128)(2,1)} %k_ref.1) | copy-start | bytes 393220

commit v6 on v5

v6 whole, which is shorter than its diff:
```python
import functools

import jax
import jax.numpy as jnp
from jax import lax
from jax.experimental import pallas as pl
from jax.experimental.pallas import tpu as pltpu
from jax.sharding import PartitionSpec as P

NN = (((1,), (0,)), ((), ()))
NT = (((1,), (1,)), ((), ()))
LANES = 128


def product(left, right, form=NN):
    return lax.dot_general(left, right, form, preferred_element_type=jnp.float32)


def head_lanes(shape, head, width):
    lane = lax.broadcasted_iota(jnp.int32, shape, len(shape) - 1)
    return (lane >= head * width) & (lane < (head + 1) * width)


def only_head(array, head, width):
    return jnp.where(head_lanes(array.shape, head, width), array, jnp.zeros_like(array))


def spread_rows(spread_ref, array):
    for piece in range(array.shape[1] // LANES):
        spread_ref[piece] = array[:, piece * LANES : (piece + 1) * LANES]


def head_rows(spread_ref, head, heads, length):
    here = pl.ds(head, length, stride=heads)
    pieces = [spread_ref[piece, here, :] for piece in range(spread_ref.shape[0])]
    return pieces[0] if len(pieces) == 1 else jnp.concatenate(pieces, axis=1)


def keep_head_rows(spread_ref, head, heads, array):
    length = array.shape[0]
    for piece in range(spread_ref.shape[0]):
        lanes = array[:, piece * LANES : (piece + 1) * LANES]
        spread_ref[piece, pl.ds(head, length, stride=heads), :] = lanes


def reordered(array, order, size):
    return jnp.concatenate([array[start : start + size] for start in order], 0)


def load_kernel(bias_ref, copies_ref, *, rows, heads):
    half = heads // 2
    order = [row * heads + part * half for part in range(2) for row in range(rows)]
    block = reordered(bias_ref[...].astype(jnp.float32), order, half).astype(copies_ref.dtype)
    copies_ref[...] = jnp.broadcast_to(block[None], copies_ref.shape)


def store_kernel(
    received_ref, dq_ref, dk_ref, dv_ref, sum_hbm, dq_hbm, dk_hbm, dv_hbm, sum_ref, sems,
    *, rows, heads
):
    pairs = ((dq_ref, dq_hbm), (dk_ref, dk_hbm), (dv_ref, dv_hbm), (sum_ref, sum_hbm))
    moves = [pltpu.make_async_copy(a, b, sems.at[n]) for n, (a, b) in enumerate(pairs)]
    for move in moves[:3]:
        move.start()
    half = heads // 2
    total = jnp.sum(received_ref[...].astype(jnp.float32), axis=0)
    order = [
        ((1 - part) * rows + row) * half for row in range(rows) for part in range(2)
    ]
    sum_ref[...] = reordered(total, order, half)
    moves[3].start()
    for move in moves:
        move.wait()


def identity(length, dtype):
    rows = lax.broadcasted_iota(jnp.int32, (length, length), 0)
    columns = lax.broadcasted_iota(jnp.int32, (length, length), 1)
    return jnp.where(rows == columns, 1.0, 0.0).astype(dtype)


def joined(parts, width):
    total = parts[0]
    for head in range(1, len(parts)):
        total = jnp.where(head_lanes(total.shape, head, width), parts[head], total)
    return total

def half_kernel(
    bias_ref, q_ref, k_ref, v_ref, g_ref, norm_ref, *refs, heads, first
):
    dqt_before, dk_before, dv_before = (None,) * 3 if first else refs[:3]
    part_ref, dq_ref, dk_ref, dv_ref, spread_ref, kt_ref = refs if first else refs[3:]
    rows, length, channels = q_ref.shape
    width = channels // heads
    half = heads // 2
    scale = width ** (-0.5)
    low = jnp.bfloat16
    every = range(half)
    eye = identity(length, low)
    core = lax.rem(lax.axis_index("row"), 2)
    base = (core if first else 1 - core) * half

    def cut(array, place):
        return array[place * length : (place + 1) * length]

    def stack(array):
        return jnp.concatenate([only_head(array, base + place, width) for place in every], 0)

    spread_rows(spread_ref, bias_ref[...].astype(jnp.float32))
    rows_of = [head_rows(spread_ref, place, half, length).astype(low) for place in every]
    turned = product(eye, jnp.concatenate(rows_of, 0), NT)
    logits = [turned[:, place * length : (place + 1) * length] for place in every]
    sums = [None] * half

    def scored(row):
        return (
            product(stack(k_ref[row]), q_ref[row], NT),
            product(stack(v_ref[row]), g_ref[row], NT),
        )

    def mixed(parts):
        total = parts[0]
        for place in range(1, half):
            lanes = head_lanes(total.shape, base + place, width)
            total = jnp.where(lanes, parts[place], total)
        return total

    depth = min(2, rows)
    ahead = [scored(row) for row in range(depth)]
    for row in range(rows):
        if row + depth < rows:
            ahead.append(scored(row + depth))
        q, g = q_ref[row], g_ref[row]
        s_all, p_all = ahead[row]
        kt_ref[row] = jnp.transpose(k_ref[row])
        w_low, s_low = [], []
        for place in every:
            norms = norm_ref[pl.ds(row * heads + base + place, 1), :]
            weights = jnp.exp(cut(s_all, place) * scale + (logits[place] - norms))
            slopes = cut(p_all, place)
            centre = jnp.sum(weights * slopes, axis=0, keepdims=True)
            grads = weights * (slopes - centre)
            sums[place] = grads if row == 0 else sums[place] + grads
            if row == rows - 1:
                upright = jnp.transpose(sums[place].astype(low)).astype(jnp.float32)
                keep_head_rows(spread_ref, place, half, upright)
            w_low.append(weights.astype(low))
            s_low.append(grads.astype(low))
        dk_all = product(jnp.concatenate(s_low, 0), q)
        dv_all = product(jnp.concatenate(w_low, 0), g)
        dk = (mixed([cut(dk_all, place) for place in every]) * scale).astype(low)
        dv = mixed([cut(dv_all, place) for place in every]).astype(low)
        dqt = []
        for place in every:
            mine = pl.ds(pl.multiple_of((base + place) * width, width), width)
            dqt.append(product(kt_ref[row, mine, :], s_low[place]))
        dqt = (jnp.concatenate(dqt, 0) * scale).astype(low)
        if first:
            dq_ref[row] = dqt
        else:
            lanes = lax.broadcasted_iota(jnp.int32, dk.shape, 1)
            now = (lanes >= base * width) & (lanes < (base + half) * width)
            dk = jnp.where(now, dk, dk_before[row])
            dv = jnp.where(now, dv, dv_before[row])
            before = dqt_before[row]
            low_part = jnp.where(base == 0, dqt, before)
            high_part = jnp.where(base == 0, before, dqt)
            dq_ref[row] = jnp.transpose(jnp.concatenate([low_part, high_part], 0))
        dk_ref[row] = dk
        dv_ref[row] = dv
    for piece in range(length // LANES):
        lanes = spread_ref[piece].astype(part_ref.dtype)
        part_ref[:, piece * LANES : (piece + 1) * LANES] = lanes


def call(kernel, name, outputs, scratch=(), ins=None, outs=None, cost=None):
    def place(space):
        return pl.BlockSpec(memory_space=space)

    specs = {}
    if ins is not None:
        specs["in_specs"] = [place(space) for space in ins]
    if outs is not None:
        specs["out_specs"] = tuple(place(space) for space in outs)
    return pl.pallas_call(
        kernel,
        name=name,
        cost_estimate=cost,
        out_shape=outputs,
        scratch_shapes=scratch,
        compiler_params=pltpu.CompilerParams(vmem_limit_bytes=24 << 20),
        **specs,
    )


def local(queries, keys, values, grads_out, log_norm, bias):
    heads = bias.shape[1]
    rows, length, channels = queries.shape
    devices = lax.axis_size("row")
    shape, f32, bf16 = jax.ShapeDtypeStruct, jnp.float32, jnp.bfloat16
    hbm, vmem, dma = pltpu.HBM, pltpu.VMEM, pltpu.SemaphoreType.DMA
    half = heads // 2
    block = (rows * heads, length)
    flat = (devices * rows * half, length)
    parcel = (devices, rows * half, length)
    chips = (devices // 2,) + block
    pair = shape(queries.shape, bf16)
    sizes = dict(rows=rows, heads=heads)
    siblings = [(device, device ^ 1) for device in range(devices)]
    copies = call(
        functools.partial(load_kernel, **sizes),
        "load",
        shape(chips, bf16),
        cost=pl.CostEstimate(flops=1 << 34, bytes_accessed=1 << 26, transcendentals=0),
    )(bias.reshape(block))
    mine = lax.all_to_all(copies.reshape(parcel), "row", 0, 0).reshape(flat)
    other = lax.ppermute(mine, "row", siblings)
    saved = (queries, keys, values, grads_out, log_norm.reshape(block))
    scratch = (
        vmem((length // LANES, length * half, LANES), f32),
        vmem((rows, channels, length), bf16),
    )
    part, *before = call(
        functools.partial(half_kernel, heads=heads, first=True),
        "first",
        (shape(flat, bf16), shape((rows, channels // 2, length), bf16), pair, pair),
        scratch,
        cost=pl.CostEstimate(flops=1 << 30, bytes_accessed=1 << 20, transcendentals=0),
    )(mine, *saved)
    theirs = lax.ppermute(part, "row", siblings)
    part, *grads = call(
        functools.partial(half_kernel, heads=heads, first=False),
        "second",
        (shape(flat, f32),) + (pair,) * 3,
        scratch,
        cost=pl.CostEstimate(flops=1 << 30, bytes_accessed=1 << 20, transcendentals=0),
    )(other, *saved, *before)
    both = (part + theirs.astype(f32)).astype(bf16)
    received = lax.all_to_all(both.reshape(parcel), "row", 0, 0).reshape(chips)
    bias_grad, *grads = call(
        functools.partial(store_kernel, **sizes),
        "store",
        (shape(block, f32),) + (pair,) * 3,
        (vmem(block, f32), dma((4,))),
        (vmem,) * 4,
        (hbm,) * 4,
    )(received, *grads)
    return (*grads, bias_grad.reshape(bias.shape))


def solution(mesh):
    placed = P(("crop", "row"), None, None)
    return jax.shard_map(
        local, mesh=mesh, in_specs=(placed,) * 6, out_specs=(placed,) * 4, check_vma=False
    )
```

time: 28.8 us -> 28.2 us (0.979)
  blocking collectives: 25.3 us -> 23.6 us
  starting transfers between devices: 0 us -> 0.57 us
  Pallas kernels: 1.9 us -> 2.2 us
    all_to_all x2, blocking collectives: 25.3 us -> 23.6 us  [the longest x1 14.5 us: local(): mine = lax.all_to_all(copies.reshape(parcel), 'row', 0, 0).reshape(flat)]
    ppermute x0 -> x2, starting transfers between devices: none -> 0.57 us  [the longest x1 0.46 us: local(): theirs = lax.ppermute(part, 'row', siblings)]
    pallas_call x3 -> x4, Pallas kernels: 1.9 us -> 2.2 us  [the longest x1 0.78 us: local(): call(functools.partial(store_kernel, **sizes), 'store', (shape(block, f32...]
  transfers between devices with their start and end apart: 0 -> 2, of which waited for: 0 -> 1; matrix products, arithmetic and copies ran while one was open for 0% -> 0% of each run, Pallas kernels for 0% -> 5%
where the time goes in v6:
time: 28.2 us; the launch traced here: 28 us
  blocking collectives  23.6 us (84%)
  Pallas kernels  2.2 us (8%)
  local copies, waits for them, and re-layouts  0.7 us (2%)
  between operations  0.69 us (2%)
  starting transfers between devices  0.57 us (2%)
    all_to_all x1, blocking collectives, local(): mine = lax.all_to_all(copies.reshape(parcel), 'row', 0, 0).reshape(flat)  14.5 us
    all_to_all x1, blocking collectives, local(): received = lax.all_to_all(both.reshape(parcel), 'row', 0, 0).reshape(chips)  9.1 us
    pallas_call x1, Pallas kernels, local(): call(functools.partial(store_kernel, **sizes), 'store', (shape(block, f32...  0.78 us
    pallas_call x1, Pallas kernels, local(): call(functools.partial(half_kernel, heads=heads, first=False), 'second',...  0.75 us
    unnamed x12, local copies, waits for them, and re-layouts  0.7 us
    pallas_call x1, Pallas kernels, local(): call(functools.partial(half_kernel, heads=heads, first=True), 'first', (s...  0.67 us
  transfers between devices with their start and end apart: 2, of which 1 were waited for; matrix products, arithmetic and copies ran while one was open for 0% of the time, Pallas kernels for 5%

profile of v6, /device:TPU:0, one launch (start us, length us, event | category | flops | bytes accessed | tf_op | source)
XLA Modules:
  0.0 28.0 jit_solution(6716783671834328066)
XLA Ops:
  0.6 0.0 copy-start.5
  0.6 0.7 %copy-done.5 = bf16[4,4,128]{2,1,0:T(4,128)(2,1)S(1)} copy-done((bf16[4,4,128]{2,1,0:T(4,128)(2,1)S(1)}, bf16[4,4,128]{2,1,0:T(4,128)(2,1)}, u32[]{:S(2)}) %copy-start.5) | copy-done | bytes 4120
  1.3 0.0 copy-start.1
  1.3 0.0 copy-start.2
  1.3 0.0 copy-start.3
  1.3 0.0 copy-start.4
  1.3 0.0 copy-start
  1.4 14.5 %all_to_all.10 = bf16[32,8,128]{2,1,0:T(8,128)(2,1)S(1)} all-to-all(bf16[32,8,128]{2,1,0:T(8,128)(2,1)S(1)} %bitcast.11), channel_id=1, replica_groups=mesh['crop'=1,'row'=32] {'row'}, dimensions={0} | all-to-all | bytes 131072 | tf_op jit(solution)/shard_map/all_to_all | solution.py:216
  15.9 0.1 collective-permute-start
  16.0 0.0 copy-done.1
  16.0 0.0 copy-done.2
  16.0 0.0 copy-done.3
  16.0 0.0 copy-done.4
  16.0 0.0 copy-done
  16.0 0.7 %first.1 = (bf16[256,128]{1,0:T(8,128)(2,1)S(1)}, bf16[4,64,128]{2,1,0:T(8,128)(2,1)S(1)}, bf16[4,128,128]{2,1,0:T(8,128)(2,1)S(1)}, bf16[4,128,128]{2,1,0:T(8,128)(2,1)S(1)}) custom-call(bf16[256,128]{1,0:T(8,128)(2,1)S(1)} %bitcast.10, bf16[4,128,128]{2,1,0:T(8,128)(2,1)S(1)} %copy-done, bf16[4,128,128]{2,1,0:T(8,128)(2,1)S(1)} %copy-done.1, ...), custom_call_target="tpu_custom_call" | custom-call | flops 1073741824 | bytes 1048576 | tf_op jit(solution)/shard_map/first/pallas_call | solution.py:223
  16.7 0.5 %collective-permute-start.1 = (bf16[256,128]{1,0:T(8,128)(2,1)S(1)}, bf16[256,128]{1,0:T(8,128)(2,1)S(1)}, u32[]{:S(2)}, u32[]{:S(2)}) collective-permute-start(bf16[256,128]{1,0:T(8,128)(2,1)S(1)} %get-tuple-element.20), channel_id=1, source_target_pairs={{0,1},{1,0},{2,3},{3,2},{4,5},{5,4},{6,7},{7,6},{8,9},{9,8},{10,11... | collective-permute-start | bytes 196616 | tf_op jit(solution)/shard_map/ppermute | solution.py:230
  17.2 0.0 collective-permute-done.bias_ref
  17.2 0.7 %second.1 = (f32[256,128]{1,0:T(8,128)S(1)}, bf16[4,128,128]{2,1,0:T(8,128)(2,1)S(1)}, bf16[4,128,128]{2,1,0:T(8,128)(2,1)S(1)}, bf16[4,128,128]{2,1,0:T(8,128)(2,1)S(1)}) custom-call(bf16[256,128]{1,0:T(8,128)(2,1)S(1)} %collective-permute-done.bias_ref, bf16[4,128,128]{2,1,0:T(8,128)(2,1)S(1)} %copy-done, bf16[4,128,128]{2,1,0:T(8,128)(2,1)S(1)} %copy-done.1, ...), custom_call_target="tpu_custom_call" | custom-call | flops 1073741824 | bytes 1048576 | tf_op jit(solution)/shard_map/second/pallas_call | solution.py:231
  17.9 0.1 collective-permute-done.1
  18.1 9.1 %all_to_all.11 = bf16[32,8,128]{2,1,0:T(8,128)(2,1)S(1)} all-to-all(bf16[32,8,128]{2,1,0:T(8,128)(2,1)S(1)} %fusion), channel_id=1, replica_groups=mesh['crop'=1,'row'=32] {'row'}, dimensions={0} | all-to-all | bytes 131072 | tf_op jit(solution)/shard_map/all_to_all | solution.py:239
  27.2 0.8 %store.1 = (f32[16,128]{1,0:T(8,128)}, bf16[4,128,128]{2,1,0:T(8,128)(2,1)}, bf16[4,128,128]{2,1,0:T(8,128)(2,1)}, bf16[4,128,128]{2,1,0:T(8,128)(2,1)}) custom-call(bf16[16,16,128]{2,1,0:T(8,128)(2,1)S(1)} %bitcast.8, bf16[4,128,128]{2,1,0:T(8,128)(2,1)S(1)} %get-tuple-element.21.dq_ref, bf16[4,128,128]{2,1,0:T(8,128)(2,1)S(1)} %get-tuple-element.22.dk_ref, ...), custom_call_target="tpu_custom_call" | custom-call | tf_op jit(solution)/shard_map/store/pallas_call | solution.py:240
  (2 shorter events, 0.0 us)
Async XLA Ops:
  0.6 0.7 %copy-start.5 = (bf16[4,4,128]{2,1,0:T(4,128)(2,1)S(1)}, bf16[4,4,128]{2,1,0:T(4,128)(2,1)}, u32[]{:S(2)}) copy-start(bf16[4,4,128]{2,1,0:T(4,128)(2,1)} %param.11) | copy-start | bytes 12292
  1.3 14.7 %copy-start.1 = (bf16[4,128,128]{2,1,0:T(8,128)(2,1)S(1)}, bf16[4,128,128]{2,1,0:T(8,128)(2,1)}, u32[]{:S(2)}) copy-start(bf16[4,128,128]{2,1,0:T(8,128)(2,1)} %k_ref.3) | copy-start | bytes 393220
  1.3 14.7 %copy-start.2 = (bf16[4,128,128]{2,1,0:T(8,128)(2,1)S(1)}, bf16[4,128,128]{2,1,0:T(8,128)(2,1)}, u32[]{:S(2)}) copy-start(bf16[4,128,128]{2,1,0:T(8,128)(2,1)} %v_ref.3) | copy-start | bytes 393220
  1.3 14.7 %copy-start.3 = (bf16[4,128,128]{2,1,0:T(8,128)(2,1)S(1)}, bf16[4,128,128]{2,1,0:T(8,128)(2,1)}, u32[]{:S(2)}) copy-start(bf16[4,128,128]{2,1,0:T(8,128)(2,1)} %g_ref.3) | copy-start | bytes 393220
  1.3 14.7 %copy-start.4 = (f32[4,4,128]{2,1,0:T(4,128)S(1)}, f32[4,4,128]{2,1,0:T(4,128)}, u32[]{:S(2)}) copy-start(f32[4,4,128]{2,1,0:T(4,128)} %param.10) | copy-start | bytes 24580
  1.3 14.7 %copy-start = (bf16[4,128,128]{2,1,0:T(8,128)(2,1)S(1)}, bf16[4,128,128]{2,1,0:T(8,128)(2,1)}, u32[]{:S(2)}) copy-start(bf16[4,128,128]{2,1,0:T(8,128)(2,1)} %q_ref.3) | copy-start | bytes 393220
  15.9 1.3 %collective-permute-start = (bf16[256,128]{1,0:T(8,128)(2,1)S(1)}, bf16[256,128]{1,0:T(8,128)(2,1)S(1)}, u32[]{:S(2)}, u32[]{:S(2)}) collective-permute-start(bf16[256,128]{1,0:T(8,128)(2,1)S(1)} %bitcast.9), channel_id=1, source_target_pairs={{0,1},{1,0},{2,3},{3,2},{4,5},{5,4},{6,7},{7,6},{8,9},{9,8},{10,11... | collective-permute-start | bytes 196616 | tf_op jit(solution)/shard_map/ppermute | solution.py:217
  16.7 1.4 %collective-permute-start.1 = (bf16[256,128]{1,0:T(8,128)(2,1)S(1)}, bf16[256,128]{1,0:T(8,128)(2,1)S(1)}, u32[]{:S(2)}, u32[]{:S(2)}) collective-permute-start(bf16[256,128]{1,0:T(8,128)(2,1)S(1)} %get-tuple-element.20), channel_id=1, source_target_pairs={{0,1},{1,0},{2,3},{3,2},{4,5},{5,4},{6,7},{7,6},{8,9},{9,8},{10,11... | collective-permute-start | bytes 196616 | tf_op jit(solution)/shard_map/ppermute | solution.py:230

commit v7 on v6

--- a/solution.py
+++ b/solution.py
@@ -88,8 +88,11 @@
 def half_kernel(
     bias_ref, q_ref, k_ref, v_ref, g_ref, norm_ref, *refs, heads, first
 ):
-    dqt_before, dk_before, dv_before = (None,) * 3 if first else refs[:3]
-    part_ref, dq_ref, dk_ref, dv_ref, spread_ref, kt_ref = refs if first else refs[3:]
+    if first:
+        part_ref, dq_ref, dk_ref, dv_ref, w_ref, d_ref, spread_ref, kt_ref = refs
+    else:
+        dqt_before, dk_before, dv_before, w_ref, d_ref = refs[:5]
+        part_ref, dq_ref, dk_ref, dv_ref, spread_ref, kt_ref = refs[5:]
     rows, length, channels = q_ref.shape
     width = channels // heads
     half = heads // 2
@@ -98,7 +101,9 @@
     every = range(half)
     eye = identity(length, low)
     core = lax.rem(lax.axis_index("row"), 2)
-    base = (core if first else 1 - core) * half
+    base_first = core * half
+    base = base_first if first else half - base_first
+    kept = rows - w_ref.shape[0]
 
     def cut(array, place):
         return array[place * length : (place + 1) * length]
@@ -118,21 +123,30 @@
             product(stack(v_ref[row]), g_ref[row], NT),
         )
 
-    def mixed(parts):
-        total = parts[0]
+    def mixed(product_all, start):
+        total = cut(product_all, 0)
         for place in range(1, half):
-            lanes = head_lanes(total.shape, base + place, width)
-            total = jnp.where(lanes, parts[place], total)
+            lanes = head_lanes(total.shape, start + place, width)
+            total = jnp.where(lanes, cut(product_all, place), total)
         return total
 
-    depth = min(2, rows)
+    def graded(row, w_all, s_all, start):
+        dk = (mixed(product(s_all, q_ref[row]), start) * scale).astype(low)
+        dv = mixed(product(w_all, g_ref[row]), start).astype(low)
+        dqt = []
+        for place in every:
+            mine = pl.ds(pl.multiple_of((start + place) * width, width), width)
+            dqt.append(product(kt_ref[row, mine, :], cut(s_all, place)))
+        return (jnp.concatenate(dqt, 0) * scale).astype(low), dk, dv
+
+    depth = min(3, rows)
     ahead = [scored(row) for row in range(depth)]
     for row in range(rows):
         if row + depth < rows:
             ahead.append(scored(row + depth))
-        q, g = q_ref[row], g_ref[row]
         s_all, p_all = ahead[row]
-        kt_ref[row] = jnp.transpose(k_ref[row])
+        if not first or row < kept:
+            kt_ref[row] = jnp.transpose(k_ref[row])
         w_low, s_low = [], []
         for place in every:
             norms = norm_ref[pl.ds(row * heads + base + place, 1), :]
@@ -146,23 +160,24 @@
                 keep_head_rows(spread_ref, place, half, upright)
             w_low.append(weights.astype(low))
             s_low.append(grads.astype(low))
-        dk_all = product(jnp.concatenate(s_low, 0), q)
-        dv_all = product(jnp.concatenate(w_low, 0), g)
-        dk = (mixed([cut(dk_all, place) for place in every]) * scale).astype(low)
-        dv = mixed([cut(dv_all, place) for place in every]).astype(low)
-        dqt = []
-        for place in every:
-            mine = pl.ds(pl.multiple_of((base + place) * width, width), width)
-            dqt.append(product(kt_ref[row, mine, :], s_low[place]))
-        dqt = (jnp.concatenate(dqt, 0) * scale).astype(low)
+        w_all, s_all = jnp.concatenate(w_low, 0), jnp.concatenate(s_low, 0)
+        if first and row >= kept:
+            w_ref[row - kept] = w_all
+            d_ref[row - kept] = s_all
+            continue
+        dqt, dk, dv = graded(row, w_all, s_all, base)
         if first:
             dq_ref[row] = dqt
         else:
+            if row < kept:
+                before, dk_first, dv_first = dqt_before[row], dk_before[row], dv_before[row]
+            else:
+                late = row - kept
+                before, dk_first, dv_first = graded(row, w_ref[late], d_ref[late], base_first)
             lanes = lax.broadcasted_iota(jnp.int32, dk.shape, 1)
             now = (lanes >= base * width) & (lanes < (base + half) * width)
-            dk = jnp.where(now, dk, dk_before[row])
-            dv = jnp.where(now, dv, dv_before[row])
-            before = dqt_before[row]
+            dk = jnp.where(now, dk, dk_first)
+            dv = jnp.where(now, dv, dv_first)
             low_part = jnp.where(base == 0, dqt, before)
             high_part = jnp.where(base == 0, before, dqt)
             dq_ref[row] = jnp.transpose(jnp.concatenate([low_part, high_part], 0))
@@ -220,10 +235,15 @@
         vmem((length // LANES, length * half, LANES), f32),
         vmem((rows, channels, length), bf16),
     )
+    late = min(2, rows - 1)
+    kept = rows - late
+    done = [shape((kept, channels // 2, length), bf16)]
+    done += [shape((kept, length, channels), bf16)] * 2
+    held = shape((late, half * length, length), bf16)
     part, *before = call(
         functools.partial(half_kernel, heads=heads, first=True),
         "first",
-        (shape(flat, bf16), shape((rows, channels // 2, length), bf16), pair, pair),
+        (shape(flat, bf16), *done, held, held),
         scratch,
         cost=pl.CostEstimate(flops=1 << 30, bytes_accessed=1 << 20, transcendentals=0),
     )(mine, *saved)

time: 28.2 us -> 28.1 us (level)
  no operation moved by 1% of the time
where the time goes in v7:
time: 28.1 us; the launch traced here: 27.9 us
  blocking collectives  23.6 us (84%)
  Pallas kernels  2.09 us (7%)
  between operations  0.71 us (3%)
  local copies, waits for them, and re-layouts  0.7 us (2%)
  starting transfers between devices  0.57 us (2%)
    all_to_all x1, blocking collectives, local(): mine = lax.all_to_all(copies.reshape(parcel), 'row', 0, 0).reshape(flat)  14.5 us
    all_to_all x1, blocking collectives, local(): received = lax.all_to_all(both.reshape(parcel), 'row', 0, 0).reshape(chips)  9.1 us
    pallas_call x1, Pallas kernels, local(): call(functools.partial(half_kernel, heads=heads, first=False), 'second',...  0.79 us
    pallas_call x1, Pallas kernels, local(): call(functools.partial(store_kernel, **sizes), 'store', (shape(block, f32...  0.78 us
    unnamed x12, local copies, waits for them, and re-layouts  0.7 us
  transfers between devices with their start and end apart: 2, of which 1 were waited for; matrix products, arithmetic and copies ran while one was open for 0% of the time, Pallas kernels for 5%

profile of v7, /device:TPU:0, one launch (start us, length us, event | category | flops | bytes accessed | tf_op | source)
XLA Modules:
  0.0 27.9 jit_solution(3329762283069257409)
XLA Ops:
  0.6 0.0 copy-start.5
  0.6 0.7 %copy-done.5 = bf16[4,4,128]{2,1,0:T(4,128)(2,1)S(1)} copy-done((bf16[4,4,128]{2,1,0:T(4,128)(2,1)S(1)}, bf16[4,4,128]{2,1,0:T(4,128)(2,1)}, u32[]{:S(2)}) %copy-start.5) | copy-done | bytes 4120
  1.3 0.0 copy-start.1
  1.3 0.0 copy-start.2
  1.3 0.0 copy-start.3
  1.3 0.0 copy-start.4
  1.3 0.0 copy-start
  1.4 14.5 %all_to_all.10 = bf16[32,8,128]{2,1,0:T(8,128)(2,1)S(1)} all-to-all(bf16[32,8,128]{2,1,0:T(8,128)(2,1)S(1)} %bitcast.11), channel_id=1, replica_groups=mesh['crop'=1,'row'=32] {'row'}, dimensions={0} | all-to-all | bytes 131072 | tf_op jit(solution)/shard_map/all_to_all | solution.py:231
  15.9 0.1 collective-permute-start
  16.0 0.0 copy-done.1
  16.0 0.0 copy-done.2
  16.0 0.0 copy-done.3
  16.0 0.0 copy-done.4
  16.0 0.0 copy-done
  16.0 0.5 %first.1 = (bf16[256,128]{1,0:T(8,128)(2,1)S(1)}, bf16[2,64,128]{2,1,0:T(8,128)(2,1)S(1)}, bf16[2,128,128]{2,1,0:T(8,128)(2,1)S(1)}, bf16[2,128,128]{2,1,0:T(8,1...) custom-call(bf16[256,128]{1,0:T(8,128)(2,1)S(1)} %bitcast.10, ...), custom_call_target="tpu_custom_call" | custom-call | flops 1073741824 | bytes 1048576 | tf_op jit(solution)/shard_map/first/pallas_call | solution.py:243
  16.6 0.5 %collective-permute-start.1 = (bf16[256,128]{1,0:T(8,128)(2,1)S(1)}, bf16[256,128]{1,0:T(8,128)(2,1)S(1)}, u32[]{:S(2)}, u32[]{:S(2)}) collective-permute-start(bf16[256,128]{1,0:T(8,128)(2,1)S(1)} %get-tuple-element.24), channel_id=1, source_target_pairs={{0,1},{1,0},{2,3},{3,2},{4,5},{5,4},{6,7},{7,6},{8,9},{9,8},{10,11... | collective-permute-start | bytes 196616 | tf_op jit(solution)/shard_map/ppermute | solution.py:250
  17.0 0.1 collective-permute-done.bias_ref
  17.2 0.8 %second.1 = (f32[256,128]{1,0:T(8,128)S(1)}, bf16[4,128,128]{2,1,0:T(8,128)(2,1)S(1)}, bf16[4,128,128]{2,1,0:T(8,128)(2,1)S(1)}, bf16[4,128,128]{2,1,0:T(8,128)(2,1)S(1)}) custom-call(bf16[256,128]{1,0:T(8,128)(2,1)S(1)} %collective-permute-done.bias_ref, bf16[4,128,128]{2,1,0:T(8,128)(2,1)S(1)} %copy-done, bf16[4,128,128]{2,1,0:T(8,128)(2,1)S(1)} %copy-done.1, ...), custom_call_target="tpu_custom_call" | custom-call | flops 1073741824 | bytes 1048576 | tf_op jit(solution)/shard_map/second/pallas_call | solution.py:251
  18.0 0.0 collective-permute-done.1
  18.0 9.1 %all_to_all.11 = bf16[32,8,128]{2,1,0:T(8,128)(2,1)S(1)} all-to-all(bf16[32,8,128]{2,1,0:T(8,128)(2,1)S(1)} %fusion), channel_id=1, replica_groups=mesh['crop'=1,'row'=32] {'row'}, dimensions={0} | all-to-all | bytes 131072 | tf_op jit(solution)/shard_map/all_to_all | solution.py:259
  27.1 0.8 %store.1 = (f32[16,128]{1,0:T(8,128)}, bf16[4,128,128]{2,1,0:T(8,128)(2,1)}, bf16[4,128,128]{2,1,0:T(8,128)(2,1)}, bf16[4,128,128]{2,1,0:T(8,128)(2,1)}) custom-call(bf16[16,16,128]{2,1,0:T(8,128)(2,1)S(1)} %bitcast.8, bf16[4,128,128]{2,1,0:T(8,128)(2,1)S(1)} %get-tuple-element.25.dq_ref, bf16[4,128,128]{2,1,0:T(8,128)(2,1)S(1)} %get-tuple-element.26.dk_ref, ...), custom_call_target="tpu_custom_call" | custom-call | tf_op jit(solution)/shard_map/store/pallas_call | solution.py:260
  (2 shorter events, 0.0 us)
Async XLA Ops:
  0.6 0.7 %copy-start.5 = (bf16[4,4,128]{2,1,0:T(4,128)(2,1)S(1)}, bf16[4,4,128]{2,1,0:T(4,128)(2,1)}, u32[]{:S(2)}) copy-start(bf16[4,4,128]{2,1,0:T(4,128)(2,1)} %param.11) | copy-start | bytes 12292
  1.3 14.7 %copy-start.1 = (bf16[4,128,128]{2,1,0:T(8,128)(2,1)S(1)}, bf16[4,128,128]{2,1,0:T(8,128)(2,1)}, u32[]{:S(2)}) copy-start(bf16[4,128,128]{2,1,0:T(8,128)(2,1)} %k_ref.3) | copy-start | bytes 393220
  1.3 14.7 %copy-start.2 = (bf16[4,128,128]{2,1,0:T(8,128)(2,1)S(1)}, bf16[4,128,128]{2,1,0:T(8,128)(2,1)}, u32[]{:S(2)}) copy-start(bf16[4,128,128]{2,1,0:T(8,128)(2,1)} %v_ref.3) | copy-start | bytes 393220
  1.3 14.7 %copy-start.3 = (bf16[4,128,128]{2,1,0:T(8,128)(2,1)S(1)}, bf16[4,128,128]{2,1,0:T(8,128)(2,1)}, u32[]{:S(2)}) copy-start(bf16[4,128,128]{2,1,0:T(8,128)(2,1)} %g_ref.3) | copy-start | bytes 393220
  1.3 14.7 %copy-start.4 = (f32[4,4,128]{2,1,0:T(4,128)S(1)}, f32[4,4,128]{2,1,0:T(4,128)}, u32[]{:S(2)}) copy-start(f32[4,4,128]{2,1,0:T(4,128)} %param.10) | copy-start | bytes 24580
  1.3 14.7 %copy-start = (bf16[4,128,128]{2,1,0:T(8,128)(2,1)S(1)}, bf16[4,128,128]{2,1,0:T(8,128)(2,1)}, u32[]{:S(2)}) copy-start(bf16[4,128,128]{2,1,0:T(8,128)(2,1)} %q_ref.3) | copy-start | bytes 393220
  15.9 1.3 %collective-permute-start = (bf16[256,128]{1,0:T(8,128)(2,1)S(1)}, bf16[256,128]{1,0:T(8,128)(2,1)S(1)}, u32[]{:S(2)}, u32[]{:S(2)}) collective-permute-start(bf16[256,128]{1,0:T(8,128)(2,1)S(1)} %bitcast.9), channel_id=1, source_target_pairs={{0,1},{1,0},{2,3},{3,2},{4,5},{5,4},{6,7},{7,6},{8,9},{9,8},{10,11... | collective-permute-start | bytes 196616 | tf_op jit(solution)/shard_map/ppermute | solution.py:232
  16.6 1.4 %collective-permute-start.1 = (bf16[256,128]{1,0:T(8,128)(2,1)S(1)}, bf16[256,128]{1,0:T(8,128)(2,1)S(1)}, u32[]{:S(2)}, u32[]{:S(2)}) collective-permute-start(bf16[256,128]{1,0:T(8,128)(2,1)S(1)} %get-tuple-element.24), channel_id=1, source_target_pairs={{0,1},{1,0},{2,3},{3,2},{4,5},{5,4},{6,7},{7,6},{8,9},{9,8},{10,11... | collective-permute-start | bytes 196616 | tf_op jit(solution)/shard_map/ppermute | solution.py:250

commit v8 on v7

--- a/solution.py
+++ b/solution.py
@@ -113,8 +113,11 @@
 
     spread_rows(spread_ref, bias_ref[...].astype(jnp.float32))
     rows_of = [head_rows(spread_ref, place, half, length).astype(low) for place in every]
-    turned = product(eye, jnp.concatenate(rows_of, 0), NT)
-    logits = [turned[:, place * length : (place + 1) * length] for place in every]
+    if first:
+        logits = [jnp.transpose(rows_of[place]).astype(jnp.float32) for place in every]
+    else:
+        turned = product(eye, jnp.concatenate(rows_of, 0), NT)
+        logits = [turned[:, place * length : (place + 1) * length] for place in every]
     sums = [None] * half
 
     def scored(row):

time: 28.1 us -> 28.1 us (level)
  no operation moved by 1% of the time
where the time goes in v8:
time: 28.1 us; the launch traced here: 27.9 us
  blocking collectives  23.6 us (84%)
  Pallas kernels  2.06 us (7%)
  local copies, waits for them, and re-layouts  0.7 us (2%)
  between operations  0.7 us (2%)
  starting transfers between devices  0.57 us (2%)
    all_to_all x1, blocking collectives, local(): mine = lax.all_to_all(copies.reshape(parcel), 'row', 0, 0).reshape(flat)  14.5 us
    all_to_all x1, blocking collectives, local(): received = lax.all_to_all(both.reshape(parcel), 'row', 0, 0).reshape(chips)  9.1 us
    pallas_call x1, Pallas kernels, local(): call(functools.partial(half_kernel, heads=heads, first=False), 'second',...  0.79 us
    pallas_call x1, Pallas kernels, local(): call(functools.partial(store_kernel, **sizes), 'store', (shape(block, f32...  0.78 us
    unnamed x12, local copies, waits for them, and re-layouts  0.7 us
  transfers between devices with their start and end apart: 2, of which 1 were waited for; matrix products, arithmetic and copies ran while one was open for 0% of the time, Pallas kernels for 5%

profile of v8, /device:TPU:0, one launch (start us, length us, event | category | flops | bytes accessed | tf_op | source)
XLA Modules:
  0.0 27.9 jit_solution(1287415356398179235)
XLA Ops:
  0.6 0.0 copy-start.5
  0.6 0.7 %copy-done.5 = bf16[4,4,128]{2,1,0:T(4,128)(2,1)S(1)} copy-done((bf16[4,4,128]{2,1,0:T(4,128)(2,1)S(1)}, bf16[4,4,128]{2,1,0:T(4,128)(2,1)}, u32[]{:S(2)}) %copy-start.5) | copy-done | bytes 4120
  1.3 0.0 copy-start.1
  1.3 0.0 copy-start.2
  1.3 0.0 copy-start.3
  1.3 0.0 copy-start.4
  1.3 0.0 copy-start
  1.4 14.5 %all_to_all.10 = bf16[32,8,128]{2,1,0:T(8,128)(2,1)S(1)} all-to-all(bf16[32,8,128]{2,1,0:T(8,128)(2,1)S(1)} %bitcast.11), channel_id=1, replica_groups=mesh['crop'=1,'row'=32] {'row'}, dimensions={0} | all-to-all | bytes 131072 | tf_op jit(solution)/shard_map/all_to_all | solution.py:234
  15.9 0.1 collective-permute-start
  16.0 0.0 copy-done.1
  16.0 0.0 copy-done.2
  16.0 0.0 copy-done.3
  16.0 0.0 copy-done.4
  16.0 0.0 copy-done
  16.0 0.5 %first.1 = (bf16[256,128]{1,0:T(8,128)(2,1)S(1)}, bf16[2,64,128]{2,1,0:T(8,128)(2,1)S(1)}, bf16[2,128,128]{2,1,0:T(8,128)(2,1)S(1)}, bf16[2,128,128]{2,1,0:T(8,1...) custom-call(bf16[256,128]{1,0:T(8,128)(2,1)S(1)} %bitcast.10, ...), custom_call_target="tpu_custom_call" | custom-call | flops 1073741824 | bytes 1048576 | tf_op jit(solution)/shard_map/first/pallas_call | solution.py:246
  16.5 0.5 %collective-permute-start.1 = (bf16[256,128]{1,0:T(8,128)(2,1)S(1)}, bf16[256,128]{1,0:T(8,128)(2,1)S(1)}, u32[]{:S(2)}, u32[]{:S(2)}) collective-permute-start(bf16[256,128]{1,0:T(8,128)(2,1)S(1)} %get-tuple-element.24), channel_id=1, source_target_pairs={{0,1},{1,0},{2,3},{3,2},{4,5},{5,4},{6,7},{7,6},{8,9},{9,8},{10,11... | collective-permute-start | bytes 196616 | tf_op jit(solution)/shard_map/ppermute | solution.py:253
  17.0 0.2 collective-permute-done.bias_ref
  17.2 0.8 %second.1 = (f32[256,128]{1,0:T(8,128)S(1)}, bf16[4,128,128]{2,1,0:T(8,128)(2,1)S(1)}, bf16[4,128,128]{2,1,0:T(8,128)(2,1)S(1)}, bf16[4,128,128]{2,1,0:T(8,128)(2,1)S(1)}) custom-call(bf16[256,128]{1,0:T(8,128)(2,1)S(1)} %collective-permute-done.bias_ref, bf16[4,128,128]{2,1,0:T(8,128)(2,1)S(1)} %copy-done, bf16[4,128,128]{2,1,0:T(8,128)(2,1)S(1)} %copy-done.1, ...), custom_call_target="tpu_custom_call" | custom-call | flops 1073741824 | bytes 1048576 | tf_op jit(solution)/shard_map/second/pallas_call | solution.py:254
  18.0 0.0 collective-permute-done.1
  18.0 9.1 %all_to_all.11 = bf16[32,8,128]{2,1,0:T(8,128)(2,1)S(1)} all-to-all(bf16[32,8,128]{2,1,0:T(8,128)(2,1)S(1)} %fusion), channel_id=1, replica_groups=mesh['crop'=1,'row'=32] {'row'}, dimensions={0} | all-to-all | bytes 131072 | tf_op jit(solution)/shard_map/all_to_all | solution.py:262
  27.1 0.8 %store.1 = (f32[16,128]{1,0:T(8,128)}, bf16[4,128,128]{2,1,0:T(8,128)(2,1)}, bf16[4,128,128]{2,1,0:T(8,128)(2,1)}, bf16[4,128,128]{2,1,0:T(8,128)(2,1)}) custom-call(bf16[16,16,128]{2,1,0:T(8,128)(2,1)S(1)} %bitcast.8, bf16[4,128,128]{2,1,0:T(8,128)(2,1)S(1)} %get-tuple-element.25.dq_ref, bf16[4,128,128]{2,1,0:T(8,128)(2,1)S(1)} %get-tuple-element.26.dk_ref, ...), custom_call_target="tpu_custom_call" | custom-call | tf_op jit(solution)/shard_map/store/pallas_call | solution.py:263
  (2 shorter events, 0.0 us)
Async XLA Ops:
  0.6 0.7 %copy-start.5 = (bf16[4,4,128]{2,1,0:T(4,128)(2,1)S(1)}, bf16[4,4,128]{2,1,0:T(4,128)(2,1)}, u32[]{:S(2)}) copy-start(bf16[4,4,128]{2,1,0:T(4,128)(2,1)} %param.11) | copy-start | bytes 12292
  1.3 14.7 %copy-start.1 = (bf16[4,128,128]{2,1,0:T(8,128)(2,1)S(1)}, bf16[4,128,128]{2,1,0:T(8,128)(2,1)}, u32[]{:S(2)}) copy-start(bf16[4,128,128]{2,1,0:T(8,128)(2,1)} %k_ref.3) | copy-start | bytes 393220
  1.3 14.7 %copy-start.2 = (bf16[4,128,128]{2,1,0:T(8,128)(2,1)S(1)}, bf16[4,128,128]{2,1,0:T(8,128)(2,1)}, u32[]{:S(2)}) copy-start(bf16[4,128,128]{2,1,0:T(8,128)(2,1)} %v_ref.3) | copy-start | bytes 393220
  1.3 14.7 %copy-start.3 = (bf16[4,128,128]{2,1,0:T(8,128)(2,1)S(1)}, bf16[4,128,128]{2,1,0:T(8,128)(2,1)}, u32[]{:S(2)}) copy-start(bf16[4,128,128]{2,1,0:T(8,128)(2,1)} %g_ref.3) | copy-start | bytes 393220
  1.3 14.7 %copy-start.4 = (f32[4,4,128]{2,1,0:T(4,128)S(1)}, f32[4,4,128]{2,1,0:T(4,128)}, u32[]{:S(2)}) copy-start(f32[4,4,128]{2,1,0:T(4,128)} %param.10) | copy-start | bytes 24580
  1.3 14.7 %copy-start = (bf16[4,128,128]{2,1,0:T(8,128)(2,1)S(1)}, bf16[4,128,128]{2,1,0:T(8,128)(2,1)}, u32[]{:S(2)}) copy-start(bf16[4,128,128]{2,1,0:T(8,128)(2,1)} %q_ref.3) | copy-start | bytes 393220
  15.9 1.3 %collective-permute-start = (bf16[256,128]{1,0:T(8,128)(2,1)S(1)}, bf16[256,128]{1,0:T(8,128)(2,1)S(1)}, u32[]{:S(2)}, u32[]{:S(2)}) collective-permute-start(bf16[256,128]{1,0:T(8,128)(2,1)S(1)} %bitcast.9), channel_id=1, source_target_pairs={{0,1},{1,0},{2,3},{3,2},{4,5},{5,4},{6,7},{7,6},{8,9},{9,8},{10,11... | collective-permute-start | bytes 196616 | tf_op jit(solution)/shard_map/ppermute | solution.py:235
  16.5 1.4 %collective-permute-start.1 = (bf16[256,128]{1,0:T(8,128)(2,1)S(1)}, bf16[256,128]{1,0:T(8,128)(2,1)S(1)}, u32[]{:S(2)}, u32[]{:S(2)}) collective-permute-start(bf16[256,128]{1,0:T(8,128)(2,1)S(1)} %get-tuple-element.24), channel_id=1, source_target_pairs={{0,1},{1,0},{2,3},{3,2},{4,5},{5,4},{6,7},{7,6},{8,9},{9,8},{10,11... | collective-permute-start | bytes 196616 | tf_op jit(solution)/shard_map/ppermute | solution.py:253

commit v9 on v8

--- a/solution.py
+++ b/solution.py
@@ -238,7 +238,7 @@
         vmem((length // LANES, length * half, LANES), f32),
         vmem((rows, channels, length), bf16),
     )
-    late = min(2, rows - 1)
+    late = min(1, rows - 1)
     kept = rows - late
     done = [shape((kept, channels // 2, length), bf16)]
     done += [shape((kept, length, channels), bf16)] * 2

time: 28.1 us -> 28.1 us (level)
  no operation moved by 1% of the time
where the time goes in v9:
time: 28.1 us; the launch traced here: 27.8 us
  blocking collectives  23.6 us (84%)
  Pallas kernels  2.08 us (7%)
  local copies, waits for them, and re-layouts  0.7 us (2%)
  between operations  0.69 us (2%)
  starting transfers between devices  0.57 us (2%)
    all_to_all x1, blocking collectives, local(): mine = lax.all_to_all(copies.reshape(parcel), 'row', 0, 0).reshape(flat)  14.5 us
    all_to_all x1, blocking collectives, local(): received = lax.all_to_all(both.reshape(parcel), 'row', 0, 0).reshape(chips)  9.1 us
    pallas_call x1, Pallas kernels, local(): call(functools.partial(store_kernel, **sizes), 'store', (shape(block, f32...  0.78 us
    pallas_call x1, Pallas kernels, local(): call(functools.partial(half_kernel, heads=heads, first=False), 'second',...  0.75 us
    unnamed x12, local copies, waits for them, and re-layouts  0.7 us
  transfers between devices with their start and end apart: 2, of which 1 were waited for; matrix products, arithmetic and copies ran while one was open for 0% of the time, Pallas kernels for 5%

profile of v9, /device:TPU:0, one launch (start us, length us, event | category | flops | bytes accessed | tf_op | source)
XLA Modules:
  0.0 27.8 jit_solution(9843167654726609637)
XLA Ops:
  0.6 0.0 copy-start.5
  0.6 0.7 %copy-done.5 = bf16[4,4,128]{2,1,0:T(4,128)(2,1)S(1)} copy-done((bf16[4,4,128]{2,1,0:T(4,128)(2,1)S(1)}, bf16[4,4,128]{2,1,0:T(4,128)(2,1)}, u32[]{:S(2)}) %copy-start.5) | copy-done | bytes 4120
  1.3 0.0 copy-start.1
  1.3 0.0 copy-start.2
  1.3 0.0 copy-start.3
  1.3 0.0 copy-start.4
  1.3 0.0 copy-start
  1.4 14.5 %all_to_all.10 = bf16[32,8,128]{2,1,0:T(8,128)(2,1)S(1)} all-to-all(bf16[32,8,128]{2,1,0:T(8,128)(2,1)S(1)} %bitcast.11), channel_id=1, replica_groups=mesh['crop'=1,'row'=32] {'row'}, dimensions={0} | all-to-all | bytes 131072 | tf_op jit(solution)/shard_map/all_to_all | solution.py:234
  15.9 0.1 collective-permute-start
  16.0 0.0 copy-done.1
  16.0 0.0 copy-done.2
  16.0 0.0 copy-done.3
  16.0 0.0 copy-done.4
  16.0 0.0 copy-done
  16.0 0.5 %first.1 = (bf16[256,128]{1,0:T(8,128)(2,1)S(1)}, bf16[3,64,128]{2,1,0:T(8,128)(2,1)S(1)}, bf16[3,128,128]{2,1,0:T(8,128)(2,1)S(1)}, bf16[3,128,128]{2,1,0:T(8,1...) custom-call(bf16[256,128]{1,0:T(8,128)(2,1)S(1)} %bitcast.10, ...), custom_call_target="tpu_custom_call" | custom-call | flops 1073741824 | bytes 1048576 | tf_op jit(solution)/shard_map/first/pallas_call | solution.py:246
  16.6 0.5 %collective-permute-start.1 = (bf16[256,128]{1,0:T(8,128)(2,1)S(1)}, bf16[256,128]{1,0:T(8,128)(2,1)S(1)}, u32[]{:S(2)}, u32[]{:S(2)}) collective-permute-start(bf16[256,128]{1,0:T(8,128)(2,1)S(1)} %get-tuple-element.24), channel_id=1, source_target_pairs={{0,1},{1,0},{2,3},{3,2},{4,5},{5,4},{6,7},{7,6},{8,9},{9,8},{10,11... | collective-permute-start | bytes 196616 | tf_op jit(solution)/shard_map/ppermute | solution.py:253
  17.0 0.1 collective-permute-done.bias_ref
  17.2 0.8 %second.1 = (f32[256,128]{1,0:T(8,128)S(1)}, bf16[4,128,128]{2,1,0:T(8,128)(2,1)S(1)}, bf16[4,128,128]{2,1,0:T(8,128)(2,1)S(1)}, bf16[4,128,128]{2,1,0:T(8,128)(2,1)S(1)}) custom-call(bf16[256,128]{1,0:T(8,128)(2,1)S(1)} %collective-permute-done.bias_ref, bf16[4,128,128]{2,1,0:T(8,128)(2,1)S(1)} %copy-done, bf16[4,128,128]{2,1,0:T(8,128)(2,1)S(1)} %copy-done.1, ...), custom_call_target="tpu_custom_call" | custom-call | flops 1073741824 | bytes 1048576 | tf_op jit(solution)/shard_map/second/pallas_call | solution.py:254
  17.9 0.0 collective-permute-done.1
  18.0 9.1 %all_to_all.11 = bf16[32,8,128]{2,1,0:T(8,128)(2,1)S(1)} all-to-all(bf16[32,8,128]{2,1,0:T(8,128)(2,1)S(1)} %fusion), channel_id=1, replica_groups=mesh['crop'=1,'row'=32] {'row'}, dimensions={0} | all-to-all | bytes 131072 | tf_op jit(solution)/shard_map/all_to_all | solution.py:262
  27.1 0.8 %store.1 = (f32[16,128]{1,0:T(8,128)}, bf16[4,128,128]{2,1,0:T(8,128)(2,1)}, bf16[4,128,128]{2,1,0:T(8,128)(2,1)}, bf16[4,128,128]{2,1,0:T(8,128)(2,1)}) custom-call(bf16[16,16,128]{2,1,0:T(8,128)(2,1)S(1)} %bitcast.8, bf16[4,128,128]{2,1,0:T(8,128)(2,1)S(1)} %get-tuple-element.25.dq_ref, bf16[4,128,128]{2,1,0:T(8,128)(2,1)S(1)} %get-tuple-element.26.dk_ref, ...), custom_call_target="tpu_custom_call" | custom-call | tf_op jit(solution)/shard_map/store/pallas_call | solution.py:263
  (2 shorter events, 0.0 us)
Async XLA Ops:
  0.6 0.7 %copy-start.5 = (bf16[4,4,128]{2,1,0:T(4,128)(2,1)S(1)}, bf16[4,4,128]{2,1,0:T(4,128)(2,1)}, u32[]{:S(2)}) copy-start(bf16[4,4,128]{2,1,0:T(4,128)(2,1)} %param.11) | copy-start | bytes 12292
  1.3 14.7 %copy-start.1 = (bf16[4,128,128]{2,1,0:T(8,128)(2,1)S(1)}, bf16[4,128,128]{2,1,0:T(8,128)(2,1)}, u32[]{:S(2)}) copy-start(bf16[4,128,128]{2,1,0:T(8,128)(2,1)} %k_ref.3) | copy-start | bytes 393220
  1.3 14.7 %copy-start.2 = (bf16[4,128,128]{2,1,0:T(8,128)(2,1)S(1)}, bf16[4,128,128]{2,1,0:T(8,128)(2,1)}, u32[]{:S(2)}) copy-start(bf16[4,128,128]{2,1,0:T(8,128)(2,1)} %v_ref.3) | copy-start | bytes 393220
  1.3 14.7 %copy-start.3 = (bf16[4,128,128]{2,1,0:T(8,128)(2,1)S(1)}, bf16[4,128,128]{2,1,0:T(8,128)(2,1)}, u32[]{:S(2)}) copy-start(bf16[4,128,128]{2,1,0:T(8,128)(2,1)} %g_ref.3) | copy-start | bytes 393220
  1.3 14.7 %copy-start.4 = (f32[4,4,128]{2,1,0:T(4,128)S(1)}, f32[4,4,128]{2,1,0:T(4,128)}, u32[]{:S(2)}) copy-start(f32[4,4,128]{2,1,0:T(4,128)} %param.10) | copy-start | bytes 24580
  1.3 14.7 %copy-start = (bf16[4,128,128]{2,1,0:T(8,128)(2,1)S(1)}, bf16[4,128,128]{2,1,0:T(8,128)(2,1)}, u32[]{:S(2)}) copy-start(bf16[4,128,128]{2,1,0:T(8,128)(2,1)} %q_ref.3) | copy-start | bytes 393220
  15.9 1.3 %collective-permute-start = (bf16[256,128]{1,0:T(8,128)(2,1)S(1)}, bf16[256,128]{1,0:T(8,128)(2,1)S(1)}, u32[]{:S(2)}, u32[]{:S(2)}) collective-permute-start(bf16[256,128]{1,0:T(8,128)(2,1)S(1)} %bitcast.9), channel_id=1, source_target_pairs={{0,1},{1,0},{2,3},{3,2},{4,5},{5,4},{6,7},{7,6},{8,9},{9,8},{10,11... | collective-permute-start | bytes 196616 | tf_op jit(solution)/shard_map/ppermute | solution.py:235
  16.6 1.4 %collective-permute-start.1 = (bf16[256,128]{1,0:T(8,128)(2,1)S(1)}, bf16[256,128]{1,0:T(8,128)(2,1)S(1)}, u32[]{:S(2)}, u32[]{:S(2)}) collective-permute-start(bf16[256,128]{1,0:T(8,128)(2,1)S(1)} %get-tuple-element.24), channel_id=1, source_target_pairs={{0,1},{1,0},{2,3},{3,2},{4,5},{5,4},{6,7},{7,6},{8,9},{9,8},{10,11... | collective-permute-start | bytes 196616 | tf_op jit(solution)/shard_map/ppermute | solution.py:253

commit v10 on v9

--- a/solution.py
+++ b/solution.py
@@ -159,7 +159,8 @@
             grads = weights * (slopes - centre)
             sums[place] = grads if row == 0 else sums[place] + grads
             if row == rows - 1:
-                upright = jnp.transpose(sums[place].astype(low)).astype(jnp.float32)
+                sent = sums[place].astype(low) if first else sums[place]
+                upright = jnp.transpose(sent).astype(jnp.float32)
                 keep_head_rows(spread_ref, place, half, upright)
             w_low.append(weights.astype(low))
             s_low.append(grads.astype(low))

time: 28.1 us -> 28.1 us (level)
  no operation moved by 1% of the time
where the time goes in v10:
time: 28.1 us; the launch traced here: 27.8 us
  blocking collectives  23.6 us (84%)
  Pallas kernels  2.08 us (7%)
  local copies, waits for them, and re-layouts  0.7 us (2%)
  between operations  0.69 us (2%)
  starting transfers between devices  0.57 us (2%)
    all_to_all x1, blocking collectives, local(): mine = lax.all_to_all(copies.reshape(parcel), 'row', 0, 0).reshape(flat)  14.5 us
    all_to_all x1, blocking collectives, local(): received = lax.all_to_all(both.reshape(parcel), 'row', 0, 0).reshape(chips)  9.1 us
    pallas_call x1, Pallas kernels, local(): call(functools.partial(store_kernel, **sizes), 'store', (shape(block, f32...  0.78 us
    pallas_call x1, Pallas kernels, local(): call(functools.partial(half_kernel, heads=heads, first=False), 'second',...  0.75 us
    unnamed x12, local copies, waits for them, and re-layouts  0.7 us
  transfers between devices with their start and end apart: 2, of which 1 were waited for; matrix products, arithmetic and copies ran while one was open for 0% of the time, Pallas kernels for 5%

profile of v10, /device:TPU:0, one launch (start us, length us, event | category | flops | bytes accessed | tf_op | source)
XLA Modules:
  0.0 27.8 jit_solution(17132854974206886777)
XLA Ops:
  0.6 0.0 copy-start.5
  0.6 0.7 %copy-done.5 = bf16[4,4,128]{2,1,0:T(4,128)(2,1)S(1)} copy-done((bf16[4,4,128]{2,1,0:T(4,128)(2,1)S(1)}, bf16[4,4,128]{2,1,0:T(4,128)(2,1)}, u32[]{:S(2)}) %copy-start.5) | copy-done | bytes 4120
  1.3 0.0 copy-start.1
  1.3 0.0 copy-start.2
  1.3 0.0 copy-start.3
  1.3 0.0 copy-start.4
  1.3 0.0 copy-start
  1.4 14.5 %all_to_all.10 = bf16[32,8,128]{2,1,0:T(8,128)(2,1)S(1)} all-to-all(bf16[32,8,128]{2,1,0:T(8,128)(2,1)S(1)} %bitcast.11), channel_id=1, replica_groups=mesh['crop'=1,'row'=32] {'row'}, dimensions={0} | all-to-all | bytes 131072 | tf_op jit(solution)/shard_map/all_to_all | solution.py:235
  15.9 0.1 collective-permute-start
  16.0 0.0 copy-done.1
  16.0 0.0 copy-done.2
  16.0 0.0 copy-done.3
  16.0 0.0 copy-done.4
  16.0 0.0 copy-done
  16.0 0.5 %first.1 = (bf16[256,128]{1,0:T(8,128)(2,1)S(1)}, bf16[3,64,128]{2,1,0:T(8,128)(2,1)S(1)}, bf16[3,128,128]{2,1,0:T(8,128)(2,1)S(1)}, bf16[3,128,128]{2,1,0:T(8,1...) custom-call(bf16[256,128]{1,0:T(8,128)(2,1)S(1)} %bitcast.10, ...), custom_call_target="tpu_custom_call" | custom-call | flops 1073741824 | bytes 1048576 | tf_op jit(solution)/shard_map/first/pallas_call | solution.py:247
  16.6 0.5 %collective-permute-start.1 = (bf16[256,128]{1,0:T(8,128)(2,1)S(1)}, bf16[256,128]{1,0:T(8,128)(2,1)S(1)}, u32[]{:S(2)}, u32[]{:S(2)}) collective-permute-start(bf16[256,128]{1,0:T(8,128)(2,1)S(1)} %get-tuple-element.24), channel_id=1, source_target_pairs={{0,1},{1,0},{2,3},{3,2},{4,5},{5,4},{6,7},{7,6},{8,9},{9,8},{10,11... | collective-permute-start | bytes 196616 | tf_op jit(solution)/shard_map/ppermute | solution.py:254
  17.0 0.1 collective-permute-done.bias_ref
  17.2 0.8 %second.1 = (f32[256,128]{1,0:T(8,128)S(1)}, bf16[4,128,128]{2,1,0:T(8,128)(2,1)S(1)}, bf16[4,128,128]{2,1,0:T(8,128)(2,1)S(1)}, bf16[4,128,128]{2,1,0:T(8,128)(2,1)S(1)}) custom-call(bf16[256,128]{1,0:T(8,128)(2,1)S(1)} %collective-permute-done.bias_ref, bf16[4,128,128]{2,1,0:T(8,128)(2,1)S(1)} %copy-done, bf16[4,128,128]{2,1,0:T(8,128)(2,1)S(1)} %copy-done.1, ...), custom_call_target="tpu_custom_call" | custom-call | flops 1073741824 | bytes 1048576 | tf_op jit(solution)/shard_map/second/pallas_call | solution.py:255
  17.9 0.0 collective-permute-done.1
  18.0 9.1 %all_to_all.11 = bf16[32,8,128]{2,1,0:T(8,128)(2,1)S(1)} all-to-all(bf16[32,8,128]{2,1,0:T(8,128)(2,1)S(1)} %fusion), channel_id=1, replica_groups=mesh['crop'=1,'row'=32] {'row'}, dimensions={0} | all-to-all | bytes 131072 | tf_op jit(solution)/shard_map/all_to_all | solution.py:263
  27.1 0.8 %store.1 = (f32[16,128]{1,0:T(8,128)}, bf16[4,128,128]{2,1,0:T(8,128)(2,1)}, bf16[4,128,128]{2,1,0:T(8,128)(2,1)}, bf16[4,128,128]{2,1,0:T(8,128)(2,1)}) custom-call(bf16[16,16,128]{2,1,0:T(8,128)(2,1)S(1)} %bitcast.8, bf16[4,128,128]{2,1,0:T(8,128)(2,1)S(1)} %get-tuple-element.25.dq_ref, bf16[4,128,128]{2,1,0:T(8,128)(2,1)S(1)} %get-tuple-element.26.dk_ref, ...), custom_call_target="tpu_custom_call" | custom-call | tf_op jit(solution)/shard_map/store/pallas_call | solution.py:264
  (2 shorter events, 0.0 us)
Async XLA Ops:
  0.6 0.7 %copy-start.5 = (bf16[4,4,128]{2,1,0:T(4,128)(2,1)S(1)}, bf16[4,4,128]{2,1,0:T(4,128)(2,1)}, u32[]{:S(2)}) copy-start(bf16[4,4,128]{2,1,0:T(4,128)(2,1)} %param.11) | copy-start | bytes 12292
  1.3 14.7 %copy-start.1 = (bf16[4,128,128]{2,1,0:T(8,128)(2,1)S(1)}, bf16[4,128,128]{2,1,0:T(8,128)(2,1)}, u32[]{:S(2)}) copy-start(bf16[4,128,128]{2,1,0:T(8,128)(2,1)} %k_ref.3) | copy-start | bytes 393220
  1.3 14.7 %copy-start.2 = (bf16[4,128,128]{2,1,0:T(8,128)(2,1)S(1)}, bf16[4,128,128]{2,1,0:T(8,128)(2,1)}, u32[]{:S(2)}) copy-start(bf16[4,128,128]{2,1,0:T(8,128)(2,1)} %v_ref.3) | copy-start | bytes 393220
  1.3 14.7 %copy-start.3 = (bf16[4,128,128]{2,1,0:T(8,128)(2,1)S(1)}, bf16[4,128,128]{2,1,0:T(8,128)(2,1)}, u32[]{:S(2)}) copy-start(bf16[4,128,128]{2,1,0:T(8,128)(2,1)} %g_ref.3) | copy-start | bytes 393220
  1.3 14.7 %copy-start.4 = (f32[4,4,128]{2,1,0:T(4,128)S(1)}, f32[4,4,128]{2,1,0:T(4,128)}, u32[]{:S(2)}) copy-start(f32[4,4,128]{2,1,0:T(4,128)} %param.10) | copy-start | bytes 24580
  1.3 14.7 %copy-start = (bf16[4,128,128]{2,1,0:T(8,128)(2,1)S(1)}, bf16[4,128,128]{2,1,0:T(8,128)(2,1)}, u32[]{:S(2)}) copy-start(bf16[4,128,128]{2,1,0:T(8,128)(2,1)} %q_ref.3) | copy-start | bytes 393220
  15.9 1.3 %collective-permute-start = (bf16[256,128]{1,0:T(8,128)(2,1)S(1)}, bf16[256,128]{1,0:T(8,128)(2,1)S(1)}, u32[]{:S(2)}, u32[]{:S(2)}) collective-permute-start(bf16[256,128]{1,0:T(8,128)(2,1)S(1)} %bitcast.9), channel_id=1, source_target_pairs={{0,1},{1,0},{2,3},{3,2},{4,5},{5,4},{6,7},{7,6},{8,9},{9,8},{10,11... | collective-permute-start | bytes 196616 | tf_op jit(solution)/shard_map/ppermute | solution.py:236
  16.6 1.4 %collective-permute-start.1 = (bf16[256,128]{1,0:T(8,128)(2,1)S(1)}, bf16[256,128]{1,0:T(8,128)(2,1)S(1)}, u32[]{:S(2)}, u32[]{:S(2)}) collective-permute-start(bf16[256,128]{1,0:T(8,128)(2,1)S(1)} %get-tuple-element.24), channel_id=1, source_target_pairs={{0,1},{1,0},{2,3},{3,2},{4,5},{5,4},{6,7},{7,6},{8,9},{9,8},{10,11... | collective-permute-start | bytes 196616 | tf_op jit(solution)/shard_map/ppermute | solution.py:254
